TPU v7x, 32 devices: a whole 2x2x4 slice. The times are simulated.
32 devices in a mesh: row: 8 (over z, core), col: 4 (over y, x).
Axes of the slice: x: 2, y: 2, z: 4, core: 2. Of those that a mesh axis runs over, the one named last changes fastest.
Arguments:
- tokens: bfloat16 [24576, 1152], P(('row', 'col')), may hold values from -6 to 6
- condition: bfloat16 [6, 1152], P(None, 'row'), may hold values from -6 to 6
- clip_large: int32 [6], replicated, may hold values from 0 to 1, as said below
- modulator: bfloat16 [1152, 6, 1152], P('row', None, 'col'), may hold values from -0.1875 to 0.1875
- offsets: bfloat16 [6, 1152], P(None, 'col'), may hold values from -3 to 3
- projector: bfloat16 [1152, 3, 1152], P('row', None, 'col'), may hold values from -0.1875 to 0.1875
- priors: bfloat16 [2, 1152], P(None, 'col'), may hold values from -3 to 3
- combiner: bfloat16 [1152, 1152], P('row', 'col'), may hold values from -1.5 to 1.5
- margins: bfloat16 [1152], replicated, may hold values from -3 to 3
- expander: bfloat16 [1152, 4608], P('row', 'col'), may hold values from -0.1875 to 0.1875
- thresholds: bfloat16 [4608], P('col'), may hold values from -3 to 3
- reducer: bfloat16 [1152, 4608], P('row', 'col'), may hold values from -0.09375 to 0.09375
- baseline: bfloat16 [1152], replicated, may hold values from -3 to 3
- cotangent: bfloat16 [24576, 1152], P(('row', 'col')), may hold values from -6 to 6
Outputs:
- result: bfloat16 [24576, 1152], P(('row', 'col'))
- tokens_grad: float32 [24576, 1152], P(('row', 'col'))
- condition_grad: float32 [6, 1152], P(None, 'row')
- modulator_grad: float32 [1152, 6, 1152], P('row', None, 'col')
- offsets_grad: float32 [6, 1152], P(None, 'col')
- projector_grad: float32 [1152, 3, 1152], P('row', None, 'col')
- priors_grad: float32 [2, 1152], P(None, 'col')
- combiner_grad: float32 [1152, 1152], P('row', 'col')
- margins_grad: float32 [1152], replicated
- expander_grad: float32 [1152, 4608], P('row', 'col')
- thresholds_grad: float32 [4608], P('col')
- reducer_grad: float32 [1152, 4608], P('row', 'col')
- baseline_grad: float32 [1152], replicated
Inputs may be any that keep to these rules, and one draw needn't show every extreme that they name: `clip_large`: 1 where the clip's frames have 1024 patches, 0 where they have 256; both kinds occur in every draw.
All inputs are finite; a program needn't handle non-finite values.
Results may differ from a plain program's by a relative error of at most 0.023.
Values may be sent and summed in bfloat16 or wider, within the bound.
A program may use at most 384 MiB of HBM per device.

v0:
```python
import jax
import jax.numpy as jnp
from jax import lax
from jax.sharding import PartitionSpec as P

HEAD_DIM = 72
PATCH_SMALL = 256
PATCH_BIG = 1024
CLIP_TOK = 4096


HIGH = lax.Precision.HIGHEST
EPSILON = 1e-06
NEGATIVE = -1e30


def spread(values):
    return lax.all_gather(values, "col", axis=0, tiled=True)


def collect(values):
    return lax.psum_scatter(
        values.astype(jnp.bfloat16), "col", scatter_dimension=0, tiled=True
    ).astype(jnp.float32)


def spread_grad(values):
    return lax.all_gather(values, "col", axis=0, tiled=True)


def collect_grad(values):
    return lax.psum_scatter(
        values.astype(jnp.bfloat16), "col", scatter_dimension=0, tiled=True
    ).astype(jnp.float32)


def normalize(values):
    center = values - jnp.mean(values, axis=-1, keepdims=True)
    scaled = lax.rsqrt(jnp.mean(center * center, axis=-1, keepdims=True) + EPSILON)
    return (center * scaled, scaled)


def norm_back(grad_hat, hat_own, scaled):
    first_mean = jnp.mean(grad_hat, axis=-1, keepdims=True)
    second_mean = jnp.mean(grad_hat * hat_own, axis=-1, keepdims=True)
    return scaled * (grad_hat - first_mean - hat_own * second_mean)


def gelu_tanh(values):
    return jax.nn.gelu(values, approximate=True)


def frame_mask(large_flag, length):
    places = jnp.arange(length, dtype=jnp.int32)
    frames = jnp.where(large_flag > 0, 0, places // PATCH_SMALL)
    return frames[:, None] == frames[None, :]


def attend_slot(packed):
    queries, key_rows, values, large_flag = packed
    scores = jnp.einsum(
        "qhe,khe->hqk", queries, key_rows, preferred_element_type=jnp.float32
    ) * HEAD_DIM ** (-0.5)
    allowed = frame_mask(large_flag, queries.shape[0])
    scores = jnp.where(allowed[None], scores, NEGATIVE)
    row_peak = jnp.max(scores, axis=-1, keepdims=True)
    exp_scores = jnp.exp(scores - row_peak)
    row_total = jnp.sum(exp_scores, axis=-1, keepdims=True)
    soft_low = (exp_scores / row_total).astype(jnp.bfloat16)
    mixed_heads = jnp.einsum("hqk,khe->qhe", soft_low, values, preferred_element_type=jnp.float32)
    return (mixed_heads.astype(jnp.bfloat16), (row_peak + jnp.log(row_total))[..., 0])


def attend_back(packed):
    queries, key_rows, values, grad_mixed, logsum, large_flag = packed
    scores = jnp.einsum(
        "qhe,khe->hqk", queries, key_rows, preferred_element_type=jnp.float32
    ) * HEAD_DIM ** (-0.5)
    allowed = frame_mask(large_flag, queries.shape[0])
    soft_full = jnp.where(allowed[None], jnp.exp(scores - logsum[..., None]), 0.0)
    soft_low = soft_full.astype(jnp.bfloat16)
    grad_values = jnp.einsum(
        "hqk,qhe->khe", soft_low, grad_mixed, preferred_element_type=jnp.float32
    )
    grad_soft = jnp.einsum("qhe,khe->hqk", grad_mixed, values, preferred_element_type=jnp.float32)
    row_dot = jnp.sum(soft_full * grad_soft, axis=-1, keepdims=True)
    grad_scores = (soft_full * (grad_soft - row_dot)).astype(jnp.bfloat16)
    grad_queries = jnp.einsum(
        "hqk,khe->qhe", grad_scores, key_rows, preferred_element_type=jnp.float32
    ) * HEAD_DIM ** (-0.5)
    grad_keys = jnp.einsum(
        "hqk,qhe->khe", grad_scores, queries, preferred_element_type=jnp.float32
    ) * HEAD_DIM ** (-0.5)
    return jnp.stack([grad_queries, grad_keys, grad_values], axis=1).astype(jnp.bfloat16)


def shards(
    tokens,
    condition,
    clip_large,
    modulator,
    offsets,
    projector,
    priors,
    combiner,
    margins,
    expander,
    thresholds,
    reducer,
    baseline,
    cotangent,
):
    columns = lax.axis_size("col")
    col_index = lax.axis_index("col")
    row_index = lax.axis_index("row")
    own_rows, full_width = tokens.shape
    tok_rows = own_rows * columns
    col_width = full_width // columns
    slot_len = PATCH_BIG
    slot_count = tok_rows // slot_len
    heads_local = col_width // HEAD_DIM
    clip_count = condition.shape[0]
    ff_local = thresholds.shape[0]
    priors_float = priors.astype(jnp.float32)
    margins_float = margins.astype(jnp.float32)
    thresholds_float = thresholds.astype(jnp.float32)
    baseline_float = baseline.astype(jnp.float32)
    full_proj, full_comb, full_expand, full_reduce = (
        lax.all_gather(projector, "row", axis=0, tiled=True),
        lax.all_gather(combiner, "row", axis=0, tiled=True),
        lax.all_gather(expander, "row", axis=0, tiled=True),
        lax.all_gather(reducer, "row", axis=0, tiled=True),
    )
    cond_float = condition.astype(jnp.float32)
    activated = jax.nn.silu(cond_float)
    modulator_float = modulator.astype(jnp.float32)
    partial_mods = jnp.einsum("kd,djc->kjc", activated, modulator_float, precision=HIGH)
    own_mods = lax.psum(partial_mods, "row") + offsets.astype(jnp.float32)[None]
    all_mods = lax.all_gather(own_mods, "col", axis=2, tiled=True)
    clip_range = jnp.arange(clip_count, dtype=jnp.int32)
    slot_global = row_index * slot_count + jnp.arange(slot_count, dtype=jnp.int32)
    slot_clip = slot_global // (CLIP_TOK // PATCH_BIG)
    choose = slot_clip[:, None] == clip_range[None, :]
    slot_picker = choose.astype(jnp.float32)
    slot_mods = jnp.einsum("sk,kjd->sjd", slot_picker, all_mods, precision=HIGH)
    slot_large = jnp.sum(jnp.where(choose, clip_large[None, :], 0), axis=1)
    own_start = row_index * tok_rows + col_index * own_rows
    own_clip = (own_start + jnp.arange(own_rows, dtype=jnp.int32)) // CLIP_TOK
    row_picker = (own_clip[:, None] == clip_range[None, :]).astype(jnp.float32)
    row_mods = jnp.einsum("tk,kjd->tjd", row_picker, all_mods, precision=HIGH)

    def own_part(values):
        flat = values.reshape(tok_rows, values.shape[-1])
        return lax.dynamic_slice_in_dim(flat, col_index * own_rows, own_rows, 0)

    def forward_pass(inputs):
        token_part, mods_slot, mods_row, weight_set = inputs
        proj_rows, comb_rows, expand_rows, reduce_rows = weight_set
        gathered = spread(token_part).astype(jnp.float32).reshape(slot_count, slot_len, full_width)
        hat_one, scale_one = normalize(gathered)
        hidden_one = (hat_one * (1.0 + mods_slot[:, None, 1]) + mods_slot[:, None, 0]).astype(
            jnp.bfloat16
        )
        bias_three = jnp.stack([priors_float[0], jnp.zeros_like(priors_float[0]), priors_float[1]])
        triple = jnp.einsum(
            "spd,djc->spjc", hidden_one, proj_rows, preferred_element_type=jnp.float32
        )
        triple = (triple + bias_three).astype(jnp.bfloat16)
        head_parts = triple.reshape(slot_count, slot_len, 3, heads_local, HEAD_DIM)
        mixed_heads, logsum = lax.map(
            attend_slot, (head_parts[:, :, 0], head_parts[:, :, 1], head_parts[:, :, 2], slot_large)
        )
        mixed_heads = mixed_heads.reshape(slot_count, slot_len, col_width)
        attn_part = jnp.einsum(
            "spc,dc->spd", mixed_heads, comb_rows, preferred_element_type=jnp.float32
        )
        branch_one = collect(attn_part.reshape(tok_rows, full_width)) + margins_float
        residual = token_part.astype(jnp.float32) + mods_row[:, 2] * branch_one
        gathered_two = spread(residual.astype(jnp.bfloat16)).astype(jnp.float32)
        hat_two, scale_two = normalize(gathered_two.reshape(slot_count, slot_len, full_width))
        hidden_two = (hat_two * (1.0 + mods_slot[:, None, 4]) + mods_slot[:, None, 3]).astype(
            jnp.bfloat16
        )
        pre_act = (
            jnp.einsum("spd,df->spf", hidden_two, expand_rows, preferred_element_type=jnp.float32)
            + thresholds_float
        )
        activation = gelu_tanh(pre_act).astype(jnp.bfloat16)
        mlp_part = jnp.einsum(
            "spf,df->spd", activation, reduce_rows, preferred_element_type=jnp.float32
        )
        branch_two = collect(mlp_part.reshape(tok_rows, full_width)) + baseline_float
        layer_out = residual + mods_row[:, 5] * branch_two
        stored = (
            hat_one,
            scale_one,
            hidden_one,
            head_parts,
            mixed_heads,
            logsum,
            branch_one,
            hat_two,
            scale_two,
            hidden_two,
            pre_act,
            activation,
            branch_two,
        )
        return (layer_out, stored)

    weight_set = (full_proj, full_comb, full_expand, full_reduce)
    layer_out, stored = forward_pass((tokens, slot_mods, row_mods, weight_set))
    inputs_again = lax.optimization_barrier((tokens, slot_mods, row_mods, weight_set))
    stored = forward_pass(inputs_again)[1]
    (
        hat_one,
        scale_one,
        hidden_one,
        head_parts,
        mixed_keep,
        logsum,
        branch_one,
        hat_two,
        scale_two,
        hidden_two,
        pre_act,
        activation,
        branch_two,
    ) = stored
    grad_final = cotangent.astype(jnp.float32)
    grad_branch_two = grad_final * row_mods[:, 5]
    grad_gate_two = grad_final * branch_two
    grad_baseline = jnp.sum(grad_branch_two, axis=0)
    grad_mlp = spread_grad(grad_branch_two.astype(jnp.bfloat16)).reshape(
        slot_count, slot_len, full_width
    )
    grad_act = jnp.einsum("spd,df->spf", grad_mlp, full_reduce, preferred_element_type=jnp.float32)
    reducer_full = jnp.einsum(
        "spd,spf->df", grad_mlp, activation, preferred_element_type=jnp.float32
    )
    grad_pre = jax.vjp(gelu_tanh, pre_act)[1](grad_act)[0].astype(jnp.bfloat16)
    grad_thresholds = jnp.sum(grad_pre.astype(jnp.float32), axis=(0, 1))
    expander_full = jnp.einsum(
        "spd,spf->df", hidden_two, grad_pre, preferred_element_type=jnp.float32
    )
    hidden_two_part = jnp.einsum(
        "spf,df->spd", grad_pre, full_expand, preferred_element_type=jnp.float32
    )
    grad_hidden_two = collect_grad(hidden_two_part.reshape(tok_rows, full_width))
    hat_two_own = own_part(hat_two)
    grad_scale_two = grad_hidden_two * hat_two_own
    grad_residual = grad_final + norm_back(
        grad_hidden_two * (1.0 + row_mods[:, 4]), hat_two_own, own_part(scale_two)
    )
    grad_branch_one = grad_residual * row_mods[:, 2]
    grad_gate_one = grad_residual * branch_one
    grad_margins = jnp.sum(grad_branch_one, axis=0)
    grad_attn = spread_grad(grad_branch_one.astype(jnp.bfloat16)).reshape(
        slot_count, slot_len, full_width
    )
    grad_mixed = jnp.einsum(
        "spd,dc->spc", grad_attn, full_comb, preferred_element_type=jnp.float32
    ).astype(jnp.bfloat16)
    combiner_full = jnp.einsum(
        "spd,spc->dc", grad_attn, mixed_keep, preferred_element_type=jnp.float32
    )
    grad_heads = grad_mixed.reshape(slot_count, slot_len, heads_local, HEAD_DIM)
    grad_triple = lax.map(
        attend_back,
        (
            head_parts[:, :, 0],
            head_parts[:, :, 1],
            head_parts[:, :, 2],
            grad_heads,
            logsum,
            slot_large,
        ),
    )
    grad_triple = grad_triple.reshape(slot_count, slot_len, 3, col_width)
    triple_sums = jnp.sum(grad_triple.astype(jnp.float32), axis=(0, 1))
    projector_full = jnp.einsum(
        "spd,spjc->djc", hidden_one, grad_triple, preferred_element_type=jnp.float32
    )
    hidden_one_part = jnp.einsum(
        "spjc,djc->spd", grad_triple, full_proj, preferred_element_type=jnp.float32
    )
    grad_hidden_one = collect_grad(hidden_one_part.reshape(tok_rows, full_width))
    hat_one_own = own_part(hat_one)
    grad_scale_one = grad_hidden_one * hat_one_own
    grad_input = grad_residual + norm_back(
        grad_hidden_one * (1.0 + row_mods[:, 1]), hat_one_own, own_part(scale_one)
    )
    row_grads = jnp.stack(
        [
            grad_hidden_one,
            grad_scale_one,
            grad_gate_one,
            grad_hidden_two,
            grad_scale_two,
            grad_gate_two,
        ],
        axis=1,
    )
    clip_grads = jnp.einsum("tk,tjd->kjd", row_picker, row_grads, precision=HIGH)
    priors_wide = lax.dynamic_update_slice_in_dim(
        jnp.zeros((2, full_width), jnp.float32),
        jnp.stack([triple_sums[0], triple_sums[2]]),
        col_index * col_width,
        1,
    )
    thresholds_wide = lax.dynamic_update_slice_in_dim(
        jnp.zeros((ff_local * columns,), jnp.float32), grad_thresholds, col_index * ff_local, 0
    )
    projector_grad, combiner_grad, expander_grad, reducer_grad = (
        lax.psum_scatter(
            projector_full.astype(jnp.bfloat16), "row", scatter_dimension=0, tiled=True
        ).astype(jnp.float32),
        lax.psum_scatter(
            combiner_full.astype(jnp.bfloat16), "row", scatter_dimension=0, tiled=True
        ).astype(jnp.float32),
        lax.psum_scatter(
            expander_full.astype(jnp.bfloat16), "row", scatter_dimension=0, tiled=True
        ).astype(jnp.float32),
        lax.psum_scatter(
            reducer_full.astype(jnp.bfloat16), "row", scatter_dimension=0, tiled=True
        ).astype(jnp.float32),
    )
    small_sums = lax.psum(
        (clip_grads, priors_wide, grad_margins, thresholds_wide, grad_baseline), ("row", "col")
    )
    mod_own = lax.dynamic_slice_in_dim(small_sums[0], col_index * col_width, col_width, 2)
    modulator_grad = jnp.einsum("kd,kjc->djc", activated, mod_own, precision=HIGH)
    offsets_grad = jnp.sum(mod_own, axis=0)
    activated_grad = lax.psum(
        jnp.einsum("kjc,djc->kd", mod_own, modulator_float, precision=HIGH), "col"
    )
    condition_grad = jax.vjp(jax.nn.silu, cond_float)[1](activated_grad)[0]
    priors_grad = lax.dynamic_slice_in_dim(small_sums[1], col_index * col_width, col_width, 1)
    thresholds_grad = lax.dynamic_slice_in_dim(small_sums[3], col_index * ff_local, ff_local, 0)
    result = layer_out.astype(jnp.bfloat16)
    return (
        result,
        grad_input,
        condition_grad,
        modulator_grad,
        offsets_grad,
        projector_grad,
        priors_grad,
        combiner_grad,
        small_sums[2],
        expander_grad,
        thresholds_grad,
        reducer_grad,
        small_sums[4],
    )


def solution(mesh):
    placed = (
        P(("row", "col"), None),
        P(None, "row"),
        P(),
        P("row", None, "col"),
        P(None, "col"),
        P("row", None, "col"),
        P(None, "col"),
        P("row", "col"),
        P(),
        P("row", "col"),
        P("col"),
        P("row", "col"),
        P(),
        P(("row", "col"), None),
    )
    return jax.shard_map(
        shards,
        mesh=mesh,
        in_specs=placed,
        out_specs=(
            P(("row", "col"), None),
            P(("row", "col"), None),
            P(None, "row"),
            P("row", None, "col"),
            P(None, "col"),
            P("row", None, "col"),
            P(None, "col"),
            P("row", "col"),
            P(),
            P("row", "col"),
            P("col"),
            P("row", "col"),
            P(),
        ),
        check_vma=False,
    )
```

profile of v0, /device:TPU:0, one launch (start us, length us, event | category | flops | bytes accessed | tf_op | source)
XLA Modules:
  0.0 1623.2 jit_solution(12071034009459162652)
XLA Ops:
  11.3 33.0 %psum.49 = f32[6,6,288]{2,0,1:T(8,128)S(1)} all-reduce(f32[6,6,288]{2,0,1:T(8,128)S(1)} %fusion.182), channel_id=1, replica_groups=mesh['row'=8,'col'=4] {'row'}, use_global_device_ids=true, to_apply=%region_0.1 | all-reduce | flops 10368 | bytes 82944 | tf_op jit(solution)/shard_map/psum | solution.py:138
  44.8 38.9 %all_gather.33 = f32[6,6,1152]{1,0,2:T(8,128)} all-gather(f32[6,6,288]{1,0,2:T(8,128)S(1)} %copy.74), channel_id=1, replica_groups=mesh['row'=8,'col'=4] {'col'}, dimensions={2}, use_global_device_ids=true | all-gather | bytes 207360 | tf_op jit(solution)/shard_map/all_gather | solution.py:139
  87.6 25.8 %all_gather.36 = bf16[1152,288]{1,0:T(8,128)(2,1)} all-gather(bf16[144,288]{1,0:T(8,128)(2,1)S(1)} %copy-done.22), channel_id=1, replica_groups=mesh['row'=8,'col'=4] {'row'}, dimensions={0}, use_global_device_ids=true | all-gather | bytes 746496 | tf_op jit(solution)/shard_map/all_gather | solution.py:130
  126.6 75.4 %all-gather.20.cloned.1.call-done = bf16[3072,1152]{1,0:T(8,128)(2,1)} async-done(((bf16[768,1152]{1,0:T(8,128)(2,1)}), bf16[3072,1152]{1,0:T(8,128)(2,1)}) %all-gather.20.cloned.1.call-update) | async-done | bytes 7077904 | tf_op jit(solution)/shard_map/all_gather | solution.py:18
  240.7 51.2 %while.39 = (s32[]{:T(128)}, bf16[3,1024,4,72]{1,3,2,0:T(8,128)(2,1)S(1)}, f32[3,4,1024]{2,1,0:T(4,128)}, bf16[3,1024,4,72]{1,3,2,0:T(8,128)(2,1)}, s32[3]{0:T(1...) while((s32[]{:T(128)}, ...), condition=%wide.region_17.18_spmd, body=%wide.region_14.17_spmd.sunk | while | flops 1259639808 | bytes 57026684 | solution.py:170
  301.3 76.3 %reduce-scatter.15.cloned.1.call-done = bf16[768,1152]{1,0:T(8,128)(2,1)} async-done(((bf16[3072,1152]{1,0:T(8,128)(2,1)}), bf16[768,1152]{1,0:T(8,128)(2,1)}) %reduce-scatter.15.cloned.1.call-update) | async-done | bytes 1769488 | tf_op jit(solution)/shard_map/reduce_scatter | solution.py:22
  387.0 71.9 %all-gather.22.cloned.1.call-done = bf16[3072,1152]{1,0:T(8,128)(2,1)} async-done(((bf16[768,1152]{1,0:T(8,128)(2,1)}), bf16[3072,1152]{1,0:T(8,128)(2,1)}) %all-gather.22.cloned.1.call-update) | async-done | bytes 7077904 | tf_op jit(solution)/shard_map/all_gather | solution.py:18
  484.5 18.3 %fusion.146 = f32[3,1024,1152]{2,1,0:T(8,128)} fusion(bf16[1152,1152]{1,0:T(8,128)(2,1)} %all-gather.16.cloned.1.call-done, f32[3,1024,1152]{1,2,0:T(8,128)} %copy.88, f32[3,1152]{1,0:T(4,128)S(1)} %copy-done.39, f32[3,1152]{1,0:T(4,128)S(1)} %copy-done.37, f32[3,1024]{1,0:T(4,128)S(1)} %rsqrt.69, f32[3,1024]{1,0:T(4,128)S(1)} %div.142), kind=kOutput, calls=%fused_computation.211 | convolution fusion | flops 8171421696 | bytes 31017984 | tf_op jit(solution)/shard_map/spd,df->spf/dot_general | solution.py:185
  502.8 34.7 %all-gather.24.cloned.1.call-done = bf16[3072,1152]{1,0:T(8,128)(2,1)} async-done(((bf16[768,1152]{1,0:T(8,128)(2,1)}), bf16[3072,1152]{1,0:T(8,128)(2,1)}) %all-gather.24.cloned.1.call-update) | async-done | bytes 7077904 | tf_op jit(solution)/shard_map/all_gather | solution.py:28
  537.5 22.8 %convert_reduce_fusion = (f32[1152]{0:T(1024)}, bf16[3,1024,1152]{2,1,0:T(8,128)(2,1)S(1)}) fusion(f32[3,1024,1152]{2,1,0:T(8,128)} %fusion.146, f32[1152]{0:T(1024)S(1)} %convert_element_type.229, bf16[3,1024,1152]{2,1,0:T(8,128)(2,1)} %bitcast.404, bf16[1152,1152]{1,0:T(8,128)(2,1)} %all-gather.18.cloned.1.call-done), kind=kOutput, calls=%fused_computation.131 | convolution fusion | flops 8235121664 | bytes 30974976 | tf_op jit(solution)/shard_map/spd,df->spf/dot_general | solution.py:237
  573.9 42.2 %all-gather.10.cloned.1.call-done = bf16[3072,1152]{1,0:T(8,128)(2,1)} async-done(((bf16[768,1152]{1,0:T(8,128)(2,1)}), bf16[3072,1152]{1,0:T(8,128)(2,1)}) %all-gather.10.cloned.1.call-update) | async-done | bytes 7077904 | tf_op jit(solution)/shard_map/all_gather | solution.py:18
  638.8 57.1 %reduce-scatter.17.cloned.1.call-done = bf16[768,1152]{1,0:T(8,128)(2,1)} async-done(((bf16[3072,1152]{1,0:T(8,128)(2,1)}), bf16[768,1152]{1,0:T(8,128)(2,1)}) %reduce-scatter.17.cloned.1.call-update) | async-done | bytes 1769488 | tf_op jit(solution)/shard_map/reduce_scatter | solution.py:32
  712.8 63.0 %while.38 = (s32[]{:T(128)}, bf16[3,1024,4,72]{1,3,2,0:T(8,128)(2,1)S(1)}, bf16[3,1024,4,72]{1,3,2,0:T(8,128)(2,1)}, s32[3]{0:T(128)S(1)}, bf16[3,1024,4,72]{1,3...) while((s32[]{:T(128)}, bf16[3,1024,4,72]{1,3,2,0:T(8,128)(2,1)S(1)}, ...), condition=%wide.region_7.8_spmd, body=%wide.region_4.7_spmd.sunk | while | flops 1234479104 | bytes 38054000 | solution.py:170
  791.3 177.8 %while.40 = (s32[]{:T(128)}, bf16[3,1024,3,4,72]{1,4,3,2,0:T(8,128)(2,1)}, bf16[3,1024,4,72]{1,3,2,0:T(8,128)(2,1)}, s32[3]{0:T(128)S(1)}, bf16[3,1024,4,72]{1,3...) while((s32[]{:T(128)}, ...), condition=%wide.region_26.27_spmd, body=%wide.region_24.26_spmd.sunk | while | flops 3065484288 | bytes 238119104 | solution.py:268
  816.8 15.6 multiply_convert_fusion.5
  877.0 15.3 multiply_convert_fusion.5
  935.5 15.3 multiply_convert_fusion.5
  979.0 15.2 dot_general.144
  994.2 14.1 bitcast_convert_fusion
  1009.0 18.9 %convolution_convert_fusion.2 = bf16[3,1024,1152]{2,1,0:T(8,128)(2,1)} fusion(bf16[1152,1152]{1,0:T(8,128)(2,1)} %all-gather.18.cloned.1.call-done, f32[3,1024,1152]{2,1,0:T(8,128)} %fusion.146, f32[1152]{0:T(1024)S(1)} %copy-done.54), kind=kOutput, calls=%fused_computation.168 | convolution fusion | flops 8192655360 | bytes 23892480 | tf_op jit(solution)/shard_map/spf,df->spd/dot_general | solution.py:189
  1028.9 57.4 %reduce-scatter.19.cloned.1.call-done = bf16[768,1152]{1,0:T(8,128)(2,1)} async-done(((bf16[3072,1152]{1,0:T(8,128)(2,1)}), bf16[768,1152]{1,0:T(8,128)(2,1)}) %reduce-scatter.19.cloned.1.call-update) | async-done | bytes 1769488 | tf_op jit(solution)/shard_map/reduce_scatter | solution.py:32
  1097.0 16.4 %fusion.115 = bf16[1152,1152]{1,0:T(8,128)(2,1)} fusion(bf16[3,1024,1152]{2,1,0:T(8,128)(2,1)} %copy-done.66, f32[3,1024,1152]{1,2,0:T(8,128)} %copy.88, f32[3,1152]{1,0:T(4,128)S(1)} %copy-done.40, f32[3,1152]{1,0:T(4,128)S(1)} %copy-done.38, f32[3,1024]{1,0:T(4,128)S(1)} %copy-done.52, f32[3,1024]{1,0:T(4,128)S(1)} %copy-done.50), kind=kOutput, calls=%fused_computation.148 | convolution fusion | flops 8172748800 | bytes 23940096 | tf_op jit(solution)/shard_map/spd,spf->df/dot_general | solution.py:243
  1113.5 18.1 %fusion.116 = bf16[1152,1152]{1,0:T(8,128)(2,1)} fusion(bf16[3,1024,1152]{2,1,0:T(8,128)(2,1)} %bitcast.405, f32[3,1024,1152]{2,1,0:T(8,128)} %fusion.146, f32[1152]{0:T(1024)S(1)} %copy-done.54), kind=kOutput, calls=%fused_computation.149 | convolution fusion | flops 8190443520 | bytes 23892480 | tf_op jit(solution)/shard_map/spd,spf->df/dot_general | solution.py:238
  1139.2 15.5 bitcast_convert_fusion.1
  1186.7 58.5 %all-gather.14.cloned.1.call-done = bf16[3072,1152]{1,0:T(8,128)(2,1)} async-done(((bf16[768,1152]{1,0:T(8,128)(2,1)}), bf16[3072,1152]{1,0:T(8,128)(2,1)}) %all-gather.14.cloned.1.call-update) | async-done | bytes 7077904 | tf_op jit(solution)/shard_map/all_gather | solution.py:18
  1254.2 26.2 %convolution_convert_fusion.4 = bf16[3,1024,1152]{2,1,0:T(8,128)(2,1)} fusion(f32[1152]{0:T(1024)S(1)} %copy-done.54, f32[3,1152]{1,0:T(4,128)S(1)} %copy-done.42, f32[3,1152]{1,0:T(4,128)S(1)} %copy-done.41, f32[3,1024]{1,0:T(4,128)S(1)} %rsqrt.65, f32[3,1024]{1,0:T(4,128)S(1)} %div.135, bf16[1152,1152]{1,0:T(8,128)(2,1)} %all-gather.18.cloned.1.call-done, ...), kind=kOutput, calls=%fused_computation.170 | convolution fusion | flops 16367616000 | bytes 19521024 | tf_op jit(solution)/shard_map/spf,df->spd/dot_general | solution.py:189
  1286.9 37.2 %reduce-scatter.29.cloned.1.call-done = bf16[144,1152]{1,0:T(8,128)(2,1)} async-done(((bf16[1152,1152]{1,0:T(8,128)(2,1)}), bf16[144,1152]{1,0:T(8,128)(2,1)}) %reduce-scatter.29.cloned.1.call-update) | async-done | bytes 331792 | tf_op jit(solution)/shard_map/reduce_scatter | solution.py:324
  1329.7 28.1 %reduce-scatter.25.cloned.1.call-done = bf16[144,288]{1,0:T(8,128)(2,1)} async-done(((bf16[1152,288]{1,0:T(8,128)(2,1)}), bf16[144,288]{1,0:T(8,128)(2,1)}) %reduce-scatter.25.cloned.1.call-update) | async-done | bytes 82960 | tf_op jit(solution)/shard_map/reduce_scatter | solution.py:318
  1359.3 36.7 %reduce-scatter.23.cloned.1.call-done = bf16[144,3,288]{2,0,1:T(8,128)(2,1)} async-done(((bf16[1152,3,288]{2,0,1:T(8,128)(2,1)}), bf16[144,3,288]{2,0,1:T(8,128)(2,1)}) %reduce-scatter.23.cloned.1.call-update) | async-done | bytes 248848 | tf_op jit(solution)/shard_map/reduce_scatter | solution.py:315
  1397.9 39.3 %all-reduce = (f32[2,1152]{1,0:T(2,128)S(1)}, f32[1152]{0:T(1024)}, f32[4608]{0:T(1024)S(1)}, f32[1152]{0:T(1024)}) all-reduce(f32[2,1152]{1,0:T(2,128)S(1)} %dynamic_update_slice.33, f32[1152]{0:T(1024)S(1)} %copy-done.32, f32[4608]{0:T(1024)S(1)} %dynamic_update_slice.34, ...), channel_id=1, replica_groups=mesh['row'=8,'col'=4] {'row','col'}, use_global_device_ids=true, to_apply=%region_36.37 | all-reduce | flops 9216 | bytes 73728 | tf_op jit(solution)/shard_map/psum | solution.py:328
  1438.5 86.0 %all-reduce.3.cloned.1.call-done = f32[6,6,1152]{2,0,1:T(8,128)} async-done(((f32[6,6,1152]{2,0,1:T(8,128)}), f32[6,6,1152]{2,0,1:T(8,128)}) %all-reduce.3.cloned.1.call-update) | async-done | bytes 165904 | tf_op jit(solution)/shard_map/psum | solution.py:328
  1541.1 64.5 %reduce-scatter.13.cloned.1.call-done = bf16[768,1152]{1,0:T(8,128)(2,1)} async-done(((bf16[3072,1152]{1,0:T(8,128)(2,1)}), bf16[768,1152]{1,0:T(8,128)(2,1)}) %reduce-scatter.13.cloned.1.call-update) | async-done | bytes 1769488 | tf_op jit(solution)/shard_map/reduce_scatter | solution.py:22
  (355 shorter events, 526.3 us)
Async XLA Ops:
  7.2 118.1 %all-gather.12.cloned.1.call-start = ((), (), s32[]{:S(2)}) async-start(), calls=%async_computation.11 | async-start | bytes 2985984 | tf_op jit(solution)/shard_map/all_gather | solution.py:129
  7.9 79.6 %copy-start.22 = (bf16[144,288]{1,0:T(8,128)(2,1)S(1)}, bf16[144,288]{1,0:T(8,128)(2,1)}, u32[]{:S(2)}) copy-start(bf16[144,288]{1,0:T(8,128)(2,1)} %param.27) | copy-start | bytes 248836
  7.9 117.4 %all-gather.16.cloned.1.call-start = ((), (), s32[]{:S(2)}) async-start(), calls=%async_computation.14 | async-start | bytes 2985984 | tf_op jit(solution)/shard_map/all_gather | solution.py:131
  8.7 116.7 %all-gather.18.cloned.1.call-start = ((), (), s32[]{:S(2)}) async-start(), calls=%async_computation.15 | async-start | bytes 2985984 | tf_op jit(solution)/shard_map/all_gather | solution.py:132
  9.4 192.6 %all-gather.20.cloned.1.call-start = ((), (), s32[]{:S(2)}) async-start(), calls=%async_computation.17 | async-start | bytes 8847360 | tf_op jit(solution)/shard_map/all_gather | solution.py:18
  125.4 252.2 %reduce-scatter.15.cloned.1.call-start = ((), (), s32[]{:S(2)}) async-start(), calls=%async_computation.18 | async-start | bytes 8847360 | tf_op jit(solution)/shard_map/reduce_scatter | solution.py:22
  126.0 100.9 %copy-start.56 = (f32[3,288]{1,0:T(4,128)}, f32[3,288]{1,0:T(4,128)S(1)}, u32[]{:S(2)}) copy-start(f32[3,288]{1,0:T(4,128)S(1)} %pad_maximum_fusion) | copy-start | bytes 10372
  126.6 100.3 %copy-start.33 = (f32[3,1152]{1,0:T(4,128)}, f32[3,1152]{1,0:T(4,128)S(1)}, u32[]{:S(2)}) copy-start(f32[3,1152]{1,0:T(4,128)S(1)} %get-tuple-element.379) | copy-start | bytes 41476
  126.6 100.3 %copy-start.35 = (f32[3,1152]{1,0:T(4,128)}, f32[3,1152]{1,0:T(4,128)S(1)}, u32[]{:S(2)}) copy-start(f32[3,1152]{1,0:T(4,128)S(1)} %get-tuple-element.380) | copy-start | bytes 41476
  300.6 158.3 %all-gather.22.cloned.1.call-start = ((), (), s32[]{:S(2)}) async-start(), calls=%async_computation.19 | async-start | bytes 8847360 | tf_op jit(solution)/shard_map/all_gather | solution.py:18
  301.3 84.9 %copy-start.19 = (f32[1152]{0:T(1024)}, f32[1152]{0:T(1024)S(1)}, u32[]{:S(2)}) copy-start(f32[1152]{0:T(1024)S(1)} %convert_element_type.225) | copy-start | bytes 13828
  382.1 155.4 %all-gather.24.cloned.1.call-start = ((), (), s32[]{:S(2)}) async-start(), calls=%async_computation.20 | async-start | bytes 8847360 | tf_op jit(solution)/shard_map/all_gather | solution.py:28
  386.2 229.9 %all-gather.10.cloned.1.call-start = ((), (), s32[]{:S(2)}) async-start(), calls=%async_computation.10 | async-start | bytes 8847360 | tf_op jit(solution)/shard_map/all_gather | solution.py:18
  387.0 309.0 %reduce-scatter.17.cloned.1.call-start = ((), (), s32[]{:S(2)}) async-start(), calls=%async_computation.21 | async-start | bytes 8847360 | tf_op jit(solution)/shard_map/reduce_scatter | solution.py:32
  387.0 150.5 %copy-start.53 = (f32[1152]{0:T(1024)}, f32[1152]{0:T(1024)S(1)}, u32[]{:S(2)}) copy-start(f32[1152]{0:T(1024)S(1)} %convert_element_type.229) | copy-start | bytes 13828
  572.4 212.1 %all-gather.26.cloned.1.call-start = ((), (), s32[]{:S(2)}) async-start(), calls=%async_computation.22 | async-start | bytes 8847360 | tf_op jit(solution)/shard_map/all_gather | solution.py:28
  707.1 321.9 %reduce-scatter.11.cloned.1.call-start = ((), (), s32[]{:S(2)}) async-start(), calls=%async_computation.12 | async-start | bytes 8847360 | tf_op jit(solution)/shard_map/reduce_scatter | solution.py:22
  784.4 301.9 %reduce-scatter.19.cloned.1.call-start = ((), (), s32[]{:S(2)}) async-start(), calls=%async_computation.23 | async-start | bytes 8847360 | tf_op jit(solution)/shard_map/reduce_scatter | solution.py:32
  1008.4 161.9 %reduce-scatter.21.cloned.1.call-start = ((), (), s32[]{:S(2)}) async-start(), calls=%async_computation.24 | async-start | bytes 8847360 | tf_op jit(solution)/shard_map/reduce_scatter | solution.py:22
  1028.0 217.2 %all-gather.14.cloned.1.call-start = ((), (), s32[]{:S(2)}) async-start(), calls=%async_computation.13 | async-start | bytes 8847360 | tf_op jit(solution)/shard_map/all_gather | solution.py:18
  1097.0 188.1 %reduce-scatter.27.cloned.1.call-start = ((), (), s32[]{:S(2)}) async-start(), calls=%async_computation.28 | async-start | bytes 2985984 | tf_op jit(solution)/shard_map/reduce_scatter | solution.py:321
  1113.5 210.6 %reduce-scatter.29.cloned.1.call-start = ((), (), s32[]{:S(2)}) async-start(), calls=%async_computation.29 | async-start | bytes 2985984 | tf_op jit(solution)/shard_map/reduce_scatter | solution.py:324
  1131.6 226.1 %reduce-scatter.25.cloned.1.call-start = ((), (), s32[]{:S(2)}) async-start(), calls=%async_computation.27 | async-start | bytes 995328 | tf_op jit(solution)/shard_map/reduce_scatter | solution.py:318
  1139.1 257.0 %reduce-scatter.23.cloned.1.call-start = ((), (), s32[]{:S(2)}) async-start(), calls=%async_computation.26 | async-start | bytes 2985984 | tf_op jit(solution)/shard_map/reduce_scatter | solution.py:315
  1154.6 369.9 %all-reduce.3.cloned.1.call-start = ((), (), s32[]{:S(2)}) async-start(), calls=%async_computation.25 | async-start | bytes 442368 | tf_op jit(solution)/shard_map/psum | solution.py:328
  1186.7 418.9 %reduce-scatter.13.cloned.1.call-start = ((), (), s32[]{:S(2)}) async-start(), calls=%async_computation.16 | async-start | bytes 8847360 | tf_op jit(solution)/shard_map/reduce_scatter | solution.py:22
  1280.4 117.5 %copy-start.31 = (f32[1152]{0:T(1024)S(1)}, f32[1152]{0:T(1024)}, u32[]{:S(2)}) copy-start(f32[1152]{0:T(1024)} %get-tuple-element.306) | copy-start | bytes 13828
  1280.4 117.5 %copy-start.32 = (f32[1152]{0:T(1024)S(1)}, f32[1152]{0:T(1024)}, u32[]{:S(2)}) copy-start(f32[1152]{0:T(1024)} %get-tuple-element.307) | copy-start | bytes 13828
  1280.4 158.1 %copy-start.44 = (f32[768]{0:T(1024)S(1)}, f32[768]{0:T(1024)}, u32[]{:S(2)}) copy-start(f32[768]{0:T(1024)} %get-tuple-element.308) | copy-start | bytes 9220
  1280.4 158.1 %copy-start.43 = (f32[768]{0:T(1024)S(1)}, f32[768]{0:T(1024)}, u32[]{:S(2)}) copy-start(f32[768]{0:T(1024)} %get-tuple-element.309) | copy-start | bytes 9220
  1280.4 256.7 %copy-start.28 = (bf16[6,144]{1,0:T(8,128)(2,1)S(1)}, bf16[6,144]{1,0:T(8,128)(2,1)}, u32[]{:S(2)}) copy-start(bf16[6,144]{1,0:T(8,128)(2,1)} %param.21) | copy-start | bytes 5188
  1280.5 325.1 %copy-start.6 = (bf16[768,1152]{1,0:T(8,128)(2,1)S(1)}, bf16[768,1152]{1,0:T(8,128)(2,1)}, u32[]{:S(2)}) copy-start(bf16[768,1152]{1,0:T(8,128)(2,1)} %param.20) | copy-start | bytes 5308420
  (59 other events, 1114.9 us)
Sparse Core Ops, SparseCore 0:
  9.6 37.3 all-gather.11
  48.6 33.9 all-gather.15
  84.3 40.2 all-gather.17
  126.3 75.6 all-gather.19
  300.7 76.7 reduce-scatter.14
  382.2 76.6 all-gather.21
  460.8 76.6 all-gather.23
  539.4 76.6 all-gather.9
  619.1 76.7 reduce-scatter.16
  707.2 76.6 all-gather.25
  787.0 76.7 reduce-scatter.10
  1008.5 77.7 reduce-scatter.18
  1089.4 76.7 reduce-scatter.20
  1168.4 76.6 all-gather.13
  1247.3 37.7 reduce-scatter.26
  1287.2 36.8 reduce-scatter.28
  1326.8 30.8 reduce-scatter.24
  1360.0 36.0 reduce-scatter.22
  1402.5 121.9 all-reduce.2
  1527.7 77.7 reduce-scatter.12
where the time goes:
time: 1630 us; the launch traced here: 1620 us
  waiting for transfers between devices  733 us (45%)
  matrix products  441 us (27%)
  other arithmetic  190 us (12%)
  blocking collectives  147 us (9%)
  local copies, waits for them, and re-layouts  88.8 us (5%)
    all_gather x4, waiting for transfers between devices, spread(): return lax.all_gather(values, 'col', axis=0, tiled=True)  248 us
    reduce_scatter x4, waiting for transfers between devices, collect(): lax.psum_scatter(values.astype(jnp.bfloat16), 'col', scatter_dimension=0,...  141 us
    reduce_scatter x2, waiting for transfers between devices, collect_grad(): lax.psum_scatter(values.astype(jnp.bfloat16), 'col', scatter_dimension=0,...  115 us
    psum x1, waiting for transfers between devices, shards(): lax.psum((clip_grads, priors_wide, grad_margins, thresholds_wide, grad_ba...  86 us
    convert_element_type x3, other arithmetic, attend_back(): grad_scores = (soft_full * (grad_soft - row_dot)).astype(jnp.bfloat16)  46.2 us
    dot_general x2, matrix products, forward_pass(): jnp.einsum('spf,df->spd', activation, reduce_rows, preferred_element_type...  45.1 us
    dot_general x6, matrix products, attend_slot(): jnp.einsum('hqk,khe->qhe', soft_low, values, preferred_element_type=jnp.f...  41.1 us
    psum x1, blocking collectives, shards(): lax.psum((clip_grads, priors_wide, grad_margins, thresholds_wide, grad_ba...  39.3 us
  transfers between devices with their start and end apart: 20, of which 14 were waited for; matrix products, arithmetic and copies ran while one was open for 36% of the time, Pallas kernels for 0%

commit v1 on v0

--- a/solution.py
+++ b/solution.py
@@ -1,6 +1,10 @@
+import functools
+
 import jax
 import jax.numpy as jnp
 from jax import lax
+from jax.experimental import pallas as pl
+from jax.experimental.pallas import tpu as pltpu
 from jax.sharding import PartitionSpec as P
 
 HEAD_DIM = 72
@@ -355,6 +359,608 @@
     )
 
 
+BF = jnp.bfloat16
+F32 = jnp.float32
+GROUP = 4
+BLOCK = 256
+HALF = 512
+LOG2E = 1.4426950408889634
+SCALE2 = HEAD_DIM ** (-0.5) * LOG2E
+GELU_C = 0.7978845608028654
+GELU_A = 0.044715
+
+
+def swap(values, axis_name, bit):
+    size = lax.axis_size(axis_name)
+    return lax.ppermute(values, axis_name, [(i, i ^ bit) for i in range(size)])
+
+
+def x_swap(values):
+    return swap(values, "col", 1)
+
+
+def y_swap(values):
+    return swap(values, "col", 2)
+
+
+def core_swap(values):
+    return swap(values, "row", 1)
+
+
+def ordered(bit, own, other, axis):
+    low = jnp.where(bit == 0, own, other)
+    high = jnp.where(bit == 0, other, own)
+    return jnp.concatenate([low, high], axis=axis)
+
+
+def dot_nt(left, right):
+    return lax.dot_general(left, right, (((1,), (1,)), ((), ())), preferred_element_type=F32)
+
+
+def dot_nn(left, right):
+    return jnp.dot(left, right, preferred_element_type=F32)
+
+
+def dot_tn(left, right):
+    return lax.dot_general(left, right, (((0,), (0,)), ((), ())), preferred_element_type=F32)
+
+
+def window(head, width):
+    low = head * HEAD_DIM // 128 * 128
+    return low, min(width, -(-(head + 1) * HEAD_DIM // 128) * 128)
+
+
+def pick(values, head):
+    width = values.shape[1]
+    low, high = window(head, width)
+    at = lax.broadcasted_iota(jnp.int32, (values.shape[0], high - low), 1) + low
+    inside = (at >= head * HEAD_DIM) & (at < (head + 1) * HEAD_DIM)
+    return jnp.where(inside, values[:, low:high], jnp.zeros((), values.dtype))
+
+
+def widen(values, low, width):
+    rows, have = values.shape
+    parts = []
+    if low:
+        parts.append(jnp.zeros((rows, low), values.dtype))
+    parts.append(values)
+    if low + have < width:
+        parts.append(jnp.zeros((rows, width - low - have), values.dtype))
+    return jnp.concatenate(parts, axis=1) if len(parts) > 1 else values
+
+
+def attend_kernel(first_row, blocks, far, flag, *refs):
+    width = GROUP * HEAD_DIM
+    pitch = -(-3 * width // 128) * 128
+    if far:
+        tri, other, mix_ref, lse_ref, keys, vals = refs
+    else:
+        tri, mix_ref, lse_ref, keys, vals = refs
+    near = blocks * BLOCK
+    total = keys.shape[0]
+    large = flag[0] > 0
+    for g in range(2):
+        base = g * pitch
+        rows = pl.ds(first_row, near)
+        keys[0:near, :] = tri[rows, base : base + width]
+        vals[0:near, :] = tri[rows, base + width : base + 2 * width]
+        if far:
+            keys[near:total, :] = other[:, (1 - g) * 2 * width : (1 - g) * 2 * width + width]
+            vals[near:total, :] = other[:, (1 - g) * 2 * width + width : (2 - g) * 2 * width]
+
+        def step(i, carry, g=g, base=base):
+            out_rows = pl.ds(pl.multiple_of(i * BLOCK, BLOCK), BLOCK)
+            in_rows = pl.ds(pl.multiple_of(first_row + i * BLOCK, BLOCK), BLOCK)
+            queries = tri[in_rows, base + 2 * width : base + 3 * width]
+
+            def run(span):
+                acc = None
+                sums = []
+                for h in range(GROUP):
+                    low, high = window(h, width)
+                    scores = dot_nt(pick(queries, h), keys[span, low:high])
+                    peak = jnp.max(scores, axis=1, keepdims=True) * SCALE2
+                    weights = jnp.exp2(scores * SCALE2 - peak)
+                    denom = jnp.sum(weights, axis=1, keepdims=True)
+                    part = dot_nn(weights.astype(BF), vals[span, low:high]) / denom
+                    at = lax.broadcasted_iota(jnp.int32, part.shape, 1) + low
+                    inside = (at >= h * HEAD_DIM) & (at < (h + 1) * HEAD_DIM)
+                    part = widen(jnp.where(inside, part, 0.0), low, width)
+                    acc = part if acc is None else acc + part
+                    sums.append(jnp.broadcast_to(peak + jnp.log2(denom), (BLOCK, 32)))
+                mix_ref[out_rows, g * width : (g + 1) * width] = acc.astype(BF)
+                flipped = jnp.concatenate(sums, axis=1).T
+                for h in range(GROUP):
+                    lse_ref[g, i, h : h + 1, :] = flipped[32 * h : 32 * h + 1]
+
+            @pl.when(large)
+            def _():
+                run(pl.ds(0, total))
+
+            @pl.when(jnp.logical_not(large))
+            def _():
+                run(out_rows)
+
+            return carry
+
+        lax.fori_loop(0, blocks, step, 0)
+
+
+def attend_fast(tri, flag, first_row, blocks, other=None):
+    width = GROUP * HEAD_DIM
+    far = other is not None
+    total = blocks * BLOCK + (other.shape[0] if far else 0)
+    rows = blocks * BLOCK
+    in_vmem = pl.BlockSpec(memory_space=pltpu.VMEM)
+    ins = [tri, other] if far else [tri]
+    work = 2 * GROUP * rows * total
+    return pl.pallas_call(
+        functools.partial(attend_kernel, first_row, blocks, far),
+        out_shape=(
+            jax.ShapeDtypeStruct((rows, 2 * width), BF),
+            jax.ShapeDtypeStruct((2, blocks, GROUP, BLOCK), F32),
+        ),
+        in_specs=[pl.BlockSpec(memory_space=pltpu.SMEM)] + [in_vmem] * len(ins),
+        out_specs=(in_vmem, in_vmem),
+        scratch_shapes=[pltpu.VMEM((total, width), BF)] * 2,
+        cost_estimate=pl.CostEstimate(
+            flops=work * 1024, bytes_accessed=8 * rows * 1024, transcendentals=work
+        ),
+        name="attend_far" if far else "attend_near",
+    )(flag, *ins)
+
+
+def attend_back_kernel(first_row, blocks, far, flag, *refs):
+    width = GROUP * HEAD_DIM
+    pitch = -(-3 * width // 128) * 128
+    if far:
+        tri, other, grad, mixed, lse, out, out_far = refs[:7]
+        keys, vals, keys_t, grad_keys, grad_vals, grad_q = refs[7:]
+    else:
+        tri, grad, mixed, lse, out = refs[:5]
+        keys, vals, keys_t, grad_keys, grad_vals, grad_q = refs[5:]
+    near = blocks * BLOCK
+    total = keys.shape[0]
+    large = flag[0] > 0
+    scale = HEAD_DIM ** (-0.5)
+    for g in range(2):
+        base = g * pitch
+        rows = pl.ds(first_row, near)
+        keys[0:near, :] = tri[rows, base : base + width]
+        vals[0:near, :] = tri[rows, base + width : base + 2 * width]
+        if far:
+            keys[near:total, :] = other[:, (1 - g) * 2 * width : (1 - g) * 2 * width + width]
+            vals[near:total, :] = other[:, (1 - g) * 2 * width + width : (2 - g) * 2 * width]
+        for b in range(total // BLOCK):
+            keys_t[:, b * BLOCK : (b + 1) * BLOCK] = keys[b * BLOCK : (b + 1) * BLOCK, :].T
+        grad_keys[...] = jnp.zeros_like(grad_keys)
+        grad_vals[...] = jnp.zeros_like(grad_vals)
+
+        def step(i, carry, g=g, base=base):
+            out_rows = pl.ds(pl.multiple_of(i * BLOCK, BLOCK), BLOCK)
+            in_rows = pl.ds(pl.multiple_of(first_row + i * BLOCK, BLOCK), BLOCK)
+
+            def run(span):
+                queries = tri[in_rows, base + 2 * width : base + 3 * width]
+                grad_mix = grad[in_rows, g * width : (g + 1) * width]
+                mix = mixed[out_rows, g * width : (g + 1) * width]
+                prod = (grad_mix.astype(F32) * mix.astype(F32)).T
+                outs = []
+                for h in range(GROUP):
+                    low, high = window(h, width)
+                    q_head = pick(queries, h)
+                    g_head = pick(grad_mix, h)
+                    dot_row = jnp.sum(
+                        prod[h * HEAD_DIM : (h + 1) * HEAD_DIM], axis=0, keepdims=True
+                    )
+                    lse_row = lse[g, i, h : h + 1, :]
+                    soft = jnp.exp2(dot_nt(keys[span, low:high], q_head) * SCALE2 - lse_row)
+                    grad_soft = dot_nt(vals[span, low:high], g_head)
+                    grad_scores = (soft * (grad_soft - dot_row)).astype(BF)
+                    grad_vals[span, low:high] += dot_nn(soft.astype(BF), g_head)
+                    grad_keys[span, low:high] += dot_nn(grad_scores, q_head)
+                    top = h * HEAD_DIM // 16 * 16
+                    end = -(-(h + 1) * HEAD_DIM // 16) * 16
+                    part = dot_nn(keys_t[top:end, span], grad_scores)
+                    outs.append(part[h * HEAD_DIM - top : h * HEAD_DIM - top + HEAD_DIM])
+                grad_q[out_rows, :] = (jnp.concatenate(outs, axis=0) * scale).T.astype(BF)
+
+            @pl.when(large)
+            def _():
+                run(pl.ds(0, total))
+
+            @pl.when(jnp.logical_not(large))
+            def _():
+                run(out_rows)
+
+            return carry
+
+        lax.fori_loop(0, blocks, step, 0)
+        pad = jnp.zeros((BLOCK, pitch - 3 * width), BF)
+        for b in range(blocks):
+            at = slice(b * BLOCK, (b + 1) * BLOCK)
+            out[at, base : base + pitch] = jnp.concatenate(
+                [
+                    (grad_keys[at, :] * scale).astype(BF),
+                    grad_vals[at, :].astype(BF),
+                    grad_q[at, :],
+                    pad,
+                ],
+                axis=1,
+            )
+        if far:
+            out_far[:, g * 2 * width : (g + 1) * 2 * width] = jnp.concatenate(
+                [
+                    (grad_keys[near:total, :] * scale).astype(BF),
+                    grad_vals[near:total, :].astype(BF),
+                ],
+                axis=1,
+            )
+
+
+def attend_back_fast(tri, flag, first_row, blocks, grad, mixed, lse, other=None):
+    width = GROUP * HEAD_DIM
+    pitch = -(-3 * width // 128) * 128
+    far = other is not None
+    rows = blocks * BLOCK
+    total = rows + (other.shape[0] if far else 0)
+    in_vmem = pl.BlockSpec(memory_space=pltpu.VMEM)
+    ins = ([tri, other] if far else [tri]) + [grad, mixed, lse]
+    outs = [jax.ShapeDtypeStruct((rows, 2 * pitch), BF)]
+    if far:
+        outs.append(jax.ShapeDtypeStruct((total - rows, 4 * width), BF))
+    work = 2 * GROUP * rows * total
+    return pl.pallas_call(
+        functools.partial(attend_back_kernel, first_row, blocks, far),
+        out_shape=tuple(outs),
+        in_specs=[pl.BlockSpec(memory_space=pltpu.SMEM)] + [in_vmem] * len(ins),
+        out_specs=tuple([in_vmem] * len(outs)),
+        scratch_shapes=[
+            pltpu.VMEM((total, width), BF),
+            pltpu.VMEM((total, width), BF),
+            pltpu.VMEM((width, total), BF),
+            pltpu.VMEM((total, width), F32),
+            pltpu.VMEM((total, width), F32),
+            pltpu.VMEM((rows, width), BF),
+        ],
+        cost_estimate=pl.CostEstimate(
+            flops=work * 2560, bytes_accessed=16 * rows * 1024, transcendentals=work
+        ),
+        name="attend_back_far" if far else "attend_back_near",
+    )(flag, *ins)
+
+
+def fast_shards(
+    tokens,
+    condition,
+    clip_large,
+    modulator,
+    offsets,
+    projector,
+    priors,
+    combiner,
+    margins,
+    expander,
+    thresholds,
+    reducer,
+    baseline,
+    cotangent,
+):
+    col = lax.axis_index("col")
+    row = lax.axis_index("row")
+    x_bit, y_bit = col % 2, col // 2
+    core, z_low, z_high = row % 2, row // 2 % 2, row // 4
+    own_rows, width = tokens.shape
+    pair_rows = 2 * own_rows
+    full_rows = PATCH_BIG
+    col_width = width // 4
+    pitch = -(-3 * col_width // 128) * 128
+    clip_count = condition.shape[0]
+    ff_local = thresholds.shape[0]
+    per_clip = CLIP_TOK // PATCH_BIG
+    blocks = pair_rows // BLOCK
+    full_blocks = full_rows // BLOCK
+
+    def canonical(own, other):
+        wide = jnp.concatenate([own, other, own, other], axis=0)
+        start = (HALF * y_bit + 2 * pair_rows - own_rows * x_bit) % pair_rows
+        return lax.dynamic_slice_in_dim(wide, start, pair_rows, 0)
+
+    def own_first(values):
+        wide = jnp.concatenate([values, values], axis=0)
+        start = (own_rows * x_bit + pair_rows - HALF * y_bit) % pair_rows
+        return lax.dynamic_slice_in_dim(wide, start, pair_rows, 0)
+
+    cond_float = condition.astype(F32)
+    activated = jax.nn.silu(cond_float)
+    modulator_float = modulator.astype(F32)
+    mods = jnp.einsum("kd,djc->kjc", activated, modulator_float, precision=HIGH)
+    for bit in (1, 2, 4):
+        mods = mods + swap(mods, "row", bit)
+    mods = (mods + offsets.astype(F32)[None])[:, :, None, :]
+    mods = ordered(x_bit, mods, x_swap(mods), 2)
+    mods = ordered(y_bit, mods, y_swap(mods), 2)
+    all_mods = mods.reshape(clip_count, 6, width)
+
+    tokens_far = x_swap(tokens)
+    cot_in = lax.optimization_barrier((cotangent, tokens_far))[0]
+    cot_far = x_swap(cot_in)
+    pair_tokens = canonical(tokens, tokens_far)
+
+    slot_full = row * 3 + 2 * y_bit
+    slot_half = row * 3 + 1
+    clip_full = slot_full // per_clip
+    clip_half = slot_half // per_clip
+    mods_full = lax.dynamic_index_in_dim(all_mods, clip_full, 0, False)
+    mods_half = lax.dynamic_index_in_dim(all_mods, clip_half, 0, False)
+    flag_full = lax.dynamic_slice_in_dim(clip_large, clip_full, 1, 0)
+    flag_half = lax.dynamic_slice_in_dim(clip_large, clip_half, 1, 0)
+    is_half = (jnp.arange(blocks) >= full_blocks)[:, None, None]
+
+    def by_block(j):
+        return jnp.where(is_half, mods_half[j][None, None], mods_full[j][None, None])
+
+    own_block = (own_rows * x_bit + pair_rows - HALF * y_bit) % pair_rows // BLOCK
+    own_ids = (own_block + jnp.arange(own_rows // BLOCK)) % blocks
+    own_half = (own_ids >= full_blocks)[:, None, None]
+
+    def own_by_block(j):
+        return jnp.where(own_half, mods_half[j][None, None], mods_full[j][None, None])
+
+    def split(values):
+        return values.reshape(-1, BLOCK, values.shape[-1])
+
+    def merge(values):
+        return values.reshape(-1, values.shape[-1])
+
+    def gather(shard):
+        return lax.all_gather(shard, "row", axis=0, tiled=True)
+
+    def fetch(values, exchange):
+        rows = values.shape[0] // 2
+        part = lax.dynamic_slice_in_dim(values, core * rows, rows, 0)
+        part = exchange(part)
+        return ordered(core, part, core_swap(part), 0)
+
+    shard = jnp.concatenate(
+        [
+            projector[:, 1],
+            projector[:, 2],
+            projector[:, 0],
+            jnp.zeros((projector.shape[0], pitch - 3 * col_width), BF),
+        ],
+        axis=1,
+    )
+    proj_own = gather(shard)
+    comb_own = gather(combiner)
+    expand_own = gather(expander)
+    reduce_own = gather(reducer)
+    proj = jnp.concatenate([proj_own, fetch(proj_own, y_swap)], axis=1)
+    comb_near = jnp.concatenate([comb_own, fetch(comb_own, y_swap)], axis=1)
+    comb = jnp.concatenate([comb_near, fetch(comb_near, x_swap)], axis=1)
+    expand = jnp.concatenate([expand_own, fetch(expand_own, y_swap)], axis=1)
+    reduce = jnp.concatenate([reduce_own, fetch(reduce_own, y_swap)], axis=1)
+    priors_two = jnp.stack([priors, y_swap(priors)]).astype(F32)
+    limits = jnp.concatenate([thresholds, y_swap(thresholds)]).astype(F32)
+    bias = jnp.concatenate(
+        [
+            jnp.zeros((2, col_width), F32),
+            priors_two[:, 1],
+            priors_two[:, 0],
+            jnp.zeros((2, pitch - 3 * col_width), F32),
+        ],
+        axis=1,
+    ).reshape(1, 2 * pitch)
+
+    hat_one, scale_one = normalize(split(pair_tokens.astype(F32)))
+    hidden_one = merge((hat_one * (1.0 + by_block(1)) + by_block(0)).astype(BF))
+    triple = (dot_nn(hidden_one, proj) + bias).astype(BF)
+    kv_send = jnp.concatenate(
+        [
+            triple[full_rows:, : 2 * col_width],
+            triple[full_rows:, pitch : pitch + 2 * col_width],
+        ],
+        axis=1,
+    )
+    kv_far = y_swap(kv_send)
+    mix_full, lse_full = attend_fast(triple, flag_full, 0, full_blocks)
+    mix_half, lse_half = attend_fast(
+        triple, flag_half, full_rows, blocks - full_blocks, kv_far
+    )
+    mixed = jnp.concatenate(
+        [
+            jnp.concatenate([mix_full, x_swap(mix_full)], axis=1),
+            jnp.concatenate([mix_half, x_swap(mix_half)], axis=1),
+        ],
+        axis=0,
+    )
+    branch_one = dot_nt(mixed, comb) + margins.astype(F32)
+    residual = merge(
+        split(pair_tokens.astype(F32)) + by_block(2) * split(branch_one)
+    )
+    hat_two, scale_two = normalize(split(residual.astype(BF).astype(F32)))
+    hidden_two = merge((hat_two * (1.0 + by_block(4)) + by_block(3)).astype(BF))
+
+    pair_cot = canonical(cotangent, cot_far).astype(F32)
+    grad_mlp = merge((split(pair_cot) * by_block(5)).astype(BF))
+    grad_act = dot_nn(grad_mlp, reduce)
+    pre_act = dot_nn(hidden_two, expand) + limits
+    inner = jnp.tanh(GELU_C * (pre_act + GELU_A * pre_act * pre_act * pre_act))
+    activation = (0.5 * pre_act * (1.0 + inner)).astype(BF)
+    slope = 0.5 * (1.0 + inner) + 0.5 * pre_act * (1.0 - inner * inner) * GELU_C * (
+        1.0 + 3.0 * GELU_A * pre_act * pre_act
+    )
+    grad_pre = (grad_act * slope).astype(BF)
+    grad_limits = jnp.sum(grad_pre.astype(F32), axis=0)
+    back_two = own_first(dot_nt(grad_pre, expand).astype(BF))
+    grad_hidden_two = back_two[:own_rows].astype(F32) + x_swap(back_two[own_rows:]).astype(F32)
+    mlp_out = own_first(dot_nt(activation, reduce).astype(BF))
+    branch_two = (
+        mlp_out[:own_rows].astype(F32)
+        + x_swap(mlp_out[own_rows:]).astype(F32)
+        + baseline.astype(F32)
+    )
+    reduce_grad = dot_tn(grad_mlp, activation).astype(BF)
+    expand_grad = dot_tn(hidden_two, grad_pre).astype(BF)
+
+    residual_own = own_first(residual)[:own_rows]
+    cot_own = cotangent.astype(F32)
+    result = merge(
+        split(residual_own) + own_by_block(5) * split(branch_two)
+    ).astype(BF)
+    hat_two_own = own_first(merge(hat_two).astype(BF))[:own_rows].astype(F32)
+    scale_two_own = own_first(scale_two.reshape(pair_rows, 1))[:own_rows]
+    branch_one_own = own_first(branch_one)[:own_rows]
+    grad_residual = cot_own + norm_back(
+        merge(split(grad_hidden_two) * (1.0 + own_by_block(4))), hat_two_own, scale_two_own
+    )
+    grad_one = merge(split(grad_residual) * own_by_block(2))
+    grad_attn = grad_one.astype(BF)
+    grad_mixed = dot_nn(grad_attn, comb).astype(BF)
+    grad_mixed_far = x_swap(grad_mixed[:, 2 * col_width :])
+    grad_mix = canonical(grad_mixed[:, : 2 * col_width], grad_mixed_far)
+    mixed_own = own_first(mixed)[:own_rows]
+    comb_grad = dot_tn(grad_attn, mixed_own).astype(BF)
+
+    back_half, back_far = attend_back_fast(
+        triple,
+        flag_half,
+        full_rows,
+        blocks - full_blocks,
+        grad_mix,
+        mix_half,
+        lse_half,
+        kv_far,
+    )
+    (back_full,) = attend_back_fast(
+        triple, flag_full, 0, full_blocks, grad_mix, mix_full, lse_full
+    )
+    back_got = y_swap(back_far)
+    gap = jnp.zeros((HALF, pitch - 2 * col_width), F32)
+    back_add = jnp.concatenate(
+        [
+            back_got[:, 2 * col_width :].astype(F32),
+            gap,
+            back_got[:, : 2 * col_width].astype(F32),
+            gap,
+        ],
+        axis=1,
+    )
+    back_half = (back_half.astype(F32) + back_add).astype(BF)
+    grad_triple = jnp.concatenate([back_full, back_half], axis=0)
+    triple_sums = jnp.sum(grad_triple.astype(F32), axis=0).reshape(2, pitch)
+    back_one = dot_nt(grad_triple, proj)
+    sums_shift = jnp.sum(split(back_one), axis=1)
+    sums_scale = jnp.sum(split(back_one) * hat_one, axis=1)
+    back_one = own_first(back_one.astype(BF))
+    grad_hidden_one = back_one[:own_rows].astype(F32) + x_swap(back_one[own_rows:]).astype(F32)
+    proj_grad = dot_tn(hidden_one, grad_triple).astype(BF)
+    hat_one_own, scale_one_own = normalize(split(tokens.astype(F32)))
+    grad_input = grad_residual + norm_back(
+        merge(split(grad_hidden_one) * (1.0 + own_by_block(1))),
+        merge(hat_one_own),
+        merge(scale_one_own),
+    )
+
+    def scatter(values, wide):
+        cols = values.shape[1] // (4 if wide else 2)
+        whole = values.reshape(4, 2, values.shape[0] // 8, values.shape[1])
+        keep = lax.dynamic_index_in_dim(whole, core, 1, False)
+        send = lax.dynamic_index_in_dim(whole, 1 - core, 1, False)
+        keep = (keep.astype(F32) + core_swap(send).astype(F32)).astype(BF)
+        if wide:
+            got = x_swap(keep[:, :, 2 * cols :])
+            keep = (keep[:, :, : 2 * cols].astype(F32) + got.astype(F32)).astype(BF)
+        got = y_swap(keep[:, :, cols:])
+        keep = (keep[:, :, :cols].astype(F32) + got.astype(F32)).astype(BF)
+        keep = keep.reshape(2, 2, *keep.shape[1:])
+        mine = lax.dynamic_index_in_dim(keep, z_high, 0, False)
+        send = lax.dynamic_index_in_dim(keep, 1 - z_high, 0, False)
+        keep = (mine.astype(F32) + swap(send, "row", 4).astype(F32)).astype(BF)
+        mine = lax.dynamic_index_in_dim(keep, z_low, 0, False)
+        send = lax.dynamic_index_in_dim(keep, 1 - z_low, 0, False)
+        return mine.astype(F32) + swap(send, "row", 2).astype(F32)
+
+    reducer_grad = scatter(reduce_grad, False)
+    expander_grad = scatter(expand_grad, False)
+    combiner_grad = scatter(comb_grad, True)
+    proj_sum = scatter(proj_grad, False)
+    projector_grad = jnp.stack(
+        [
+            proj_sum[:, 2 * col_width : 3 * col_width],
+            proj_sum[:, :col_width],
+            proj_sum[:, col_width : 2 * col_width],
+        ],
+        axis=1,
+    )
+
+    def total(values):
+        for name, bit in (("row", 1), ("row", 2), ("col", 1), ("col", 2), ("row", 4)):
+            values = values + swap(values, name, bit)
+        return values
+
+    clip_range = jnp.arange(clip_count, dtype=jnp.int32)
+    pair_clip = jnp.where(jnp.arange(blocks) >= full_blocks, clip_half, clip_full)
+    own_clip = jnp.where(own_ids >= full_blocks, clip_half, clip_full)
+    pair_pick = (pair_clip[:, None] == clip_range[None]).astype(F32)
+    own_pick = (own_clip[:, None] == clip_range[None]).astype(F32)
+
+    def clip_sum(values, picker):
+        return jnp.einsum("bk,bd->kd", picker, values, precision=HIGH)
+
+    early = [
+        clip_sum(jnp.sum(split(grad_residual * branch_one_own), axis=1), own_pick),
+        clip_sum(jnp.sum(split(grad_hidden_two), axis=1), own_pick),
+        clip_sum(jnp.sum(split(grad_hidden_two * hat_two_own), axis=1), own_pick),
+        clip_sum(jnp.sum(split(cot_own * branch_two), axis=1), own_pick),
+        jnp.sum(grad_one, axis=0)[None],
+        jnp.sum(merge(split(cot_own) * own_by_block(5)), axis=0)[None],
+    ]
+    early = total(jnp.concatenate(early, axis=0))
+    late = total(
+        jnp.concatenate(
+            [clip_sum(sums_shift, pair_pick), clip_sum(sums_scale, pair_pick)], axis=0
+        )
+    )
+    rows_early = early[: 4 * clip_count].reshape(4, clip_count, width)
+    rows_late = late.reshape(2, clip_count, width)
+    grad_mods = jnp.concatenate([rows_late, rows_early], axis=0).transpose(1, 0, 2)
+    mod_own = lax.dynamic_slice_in_dim(grad_mods, col * col_width, col_width, 2)
+    modulator_grad = jnp.einsum("kd,kjc->djc", activated, mod_own, precision=HIGH)
+    offsets_grad = jnp.sum(mod_own, axis=0)
+    activated_grad = jnp.einsum("kjc,djc->kd", mod_own, modulator_float, precision=HIGH)
+    activated_grad = activated_grad + x_swap(activated_grad)
+    activated_grad = activated_grad + y_swap(activated_grad)
+    condition_grad = jax.vjp(jax.nn.silu, cond_float)[1](activated_grad)[0]
+
+    def fold(values):
+        values = values[0] + y_swap(values[1])
+        for bit in (1, 2, 4):
+            values = values + swap(values, "row", bit)
+        return values
+
+    thresholds_grad = fold(grad_limits.reshape(2, ff_local))
+    prior_sums = fold(triple_sums)
+    priors_grad = jnp.stack(
+        [prior_sums[2 * col_width : 3 * col_width], prior_sums[col_width : 2 * col_width]]
+    )
+    return (
+        result,
+        grad_input,
+        condition_grad,
+        modulator_grad,
+        offsets_grad,
+        projector_grad,
+        priors_grad,
+        combiner_grad,
+        early[4 * clip_count],
+        expander_grad,
+        thresholds_grad,
+        reducer_grad,
+        early[4 * clip_count + 1],
+    )
+
+
 def solution(mesh):
     placed = (
         P(("row", "col"), None),
@@ -372,8 +978,9 @@
         P(),
         P(("row", "col"), None),
     )
+    fits = mesh.shape["row"] == 8 and mesh.shape["col"] == 4
     return jax.shard_map(
-        shards,
+        fast_shards if fits else shards,
         mesh=mesh,
         in_specs=placed,
         out_specs=(

time: 1630 us -> 813 us (0.50)
  waiting for transfers between devices: 733 us -> 273 us
  matrix products: 441 us -> 153 us
  blocking collectives: 147 us -> 21.6 us
  starting transfers between devices: 1.6 us -> 58.7 us
  Pallas kernels: 0 us -> 56.8 us
  other arithmetic: 190 us -> 153 us
    reduce_scatter x10 -> x0, waiting for transfers between devices: 361 us -> none  [the longest x4 141 us: collect(): lax.psum_scatter(values.astype(jnp.bfloat16), 'col', scatter_dimension=0,...]
    all_gather x9 -> x3, waiting for transfers between devices: 283 us -> 9.55 us  [gather(): return lax.all_gather(shard, 'row', axis=0, tiled=True)]
    ppermute x0 -> x64, waiting for transfers between devices: none -> 263 us  [swap(): return lax.ppermute(values, axis_name, [(i, i ^ bit) for i in range(size)])]
    dot_general x45 -> x21, matrix products: 406 us -> 153 us  [the longest x4 54.9 us: dot_nt(): lax.dot_general(left, right, (((1,), (1,)), ((), ())), preferred_element_...]
    psum x1 -> x0, waiting for transfers between devices: 86 us -> none  [shards(): lax.psum((clip_grads, priors_wide, grad_margins, thresholds_wide, grad_ba...]
    psum x3 -> x0, blocking collectives: 81.8 us -> none  [the longest x1 39.3 us: shards(): lax.psum((clip_grads, priors_wide, grad_margins, thresholds_wide, grad_ba...]
    ppermute x0 -> x64, starting transfers between devices: none -> 58.6 us  [swap(): return lax.ppermute(values, axis_name, [(i, i ^ bit) for i in range(size)])]
    pallas_call x0 -> x4, Pallas kernels: none -> 56.8 us  [the longest x2 33.7 us: attend_back_fast(): pl.pallas_call(functools.partial(attend_back_kernel, first_row, blocks, f...]
  transfers between devices with their start and end apart: 20 -> 67, of which waited for: 14 -> 29; matrix products, arithmetic and copies ran while one was open for 36% -> 38% of each run, Pallas kernels for 0% -> 7%
where the time goes in v1:
time: 813 us; the launch traced here: 806 us
  waiting for transfers between devices  273 us (34%)
  other arithmetic  153 us (19%)
  matrix products  153 us (19%)
  local copies, waits for them, and re-layouts  74.6 us (9%)
  starting transfers between devices  58.7 us (7%)
  Pallas kernels  56.8 us (7%)
  blocking collectives  21.6 us (3%)
  between operations  15.5 us (2%)
    ppermute x64, waiting for transfers between devices, swap(): return lax.ppermute(values, axis_name, [(i, i ^ bit) for i in range(size)])  263 us
    ppermute x64, starting transfers between devices, swap(): return lax.ppermute(values, axis_name, [(i, i ^ bit) for i in range(size)])  58.6 us
    dot_general x4, matrix products, dot_nt(): lax.dot_general(left, right, (((1,), (1,)), ((), ())), preferred_element_...  54.9 us
    dot_general x4, matrix products, dot_nn(): return jnp.dot(left, right, preferred_element_type=F32)  52.8 us
    dot_general x4, matrix products, dot_tn(): lax.dot_general(left, right, (((0,), (0,)), ((), ())), preferred_element_...  38 us
    pallas_call x2, Pallas kernels, attend_back_fast(): pl.pallas_call(functools.partial(attend_back_kernel, first_row, blocks, f...  33.7 us
    pallas_call x2, Pallas kernels, attend_fast(): pl.pallas_call(functools.partial(attend_kernel, first_row, blocks, far),...  23 us
    all_gather x1, blocking collectives, gather(): return lax.all_gather(shard, 'row', axis=0, tiled=True)  21.6 us
  transfers between devices with their start and end apart: 67, of which 29 were waited for; matrix products, arithmetic and copies ran while one was open for 38% of the time, Pallas kernels for 7%

profile of v1, /device:TPU:0, one launch (start us, length us, event | category | flops | bytes accessed | tf_op | source)
XLA Modules:
  0.0 806.3 jit_solution(11742312142326559383)
XLA Ops:
  16.0 21.6 %all_gather.13 = bf16[1152,288]{1,0:T(8,128)(2,1)S(1)} all-gather(bf16[144,288]{1,0:T(8,128)(2,1)} %param.21), channel_id=1, replica_groups=mesh['row'=8,'col'=4] {'row'}, dimensions={0}, use_global_device_ids=true | all-gather | bytes 746496 | tf_op jit(solution)/shard_map/all_gather | solution.py:717
  79.0 10.5 %collective-permute-done.14 = bf16[576,576]{1,0:T(8,128)(2,1)} collective-permute-done((bf16[576,576]{1,0:T(8,128)(2,1)}, bf16[576,576]{1,0:T(8,128)(2,1)}, u32[]{:S(2)}, u32[]{:S(2)}) %collective-permute-start.14) | collective-permute-done | bytes 663584 | tf_op jit(solution)/shard_map/ppermute | solution.py:375
  89.8 6.4 convert_reduce_fusion.3
  106.8 9.5 %all-gather.8.cloned.1.call-done = bf16[1152,1152]{1,0:T(8,128)(2,1)} async-done(((bf16[144,1152]{1,0:T(8,128)(2,1)}), bf16[1152,1152]{1,0:T(8,128)(2,1)}) %all-gather.8.cloned.1.call-update) | async-done | bytes 2654224 | tf_op jit(solution)/shard_map/all_gather | solution.py:717
  122.0 7.5 add_convert_fusion.refs_0_
  132.3 13.4 %attend_near.1 = (bf16[1024,576]{1,0:T(8,128)(2,1)}, f32[2,4,4,256]{3,2,1,0:T(4,128)}) custom-call(s32[1]{0:T(128)} %get-tuple-element.108.flag, bf16[1536,1792]{1,0:T(8,128)(2,1)} %copy-done.48), custom_call_target="tpu_custom_call" | custom-call | flops 8589934592 | bytes 8388608 | tf_op jit(solution)/shard_map/attend_near/pallas_call | solution.py:497
  160.4 12.0 %fusion.13 = bf16[1536,1152]{1,0:T(8,128)(2,1)} fusion(s32[]{:T(128)S(6)} %select_n.337, bf16[768,1152]{1,0:T(8,128)(2,1)S(1)} %copy-done.18, bf16[768,1152]{1,0:T(8,128)(2,1)} %collective-permute-done.22, f32[6,1152]{1,0:T(8,128)S(1)} %get-tuple-element.102), kind=kLoop, calls=%fused_computation.55 | loop fusion | flops 17694720 | bytes 7105540 | tf_op jit(solution)/shard_map/convert_element_type | solution.py:785
  172.9 17.7 %collective-permute-done.10.refs_1_ = bf16[512,1152]{1,0:T(8,128)(2,1)} collective-permute-done((bf16[512,1152]{1,0:T(8,128)(2,1)}, bf16[512,1152]{1,0:T(8,128)(2,1)}, u32[]{:S(2)}, u32[]{:S(2)}) %collective-permute-start.10) | collective-permute-done | bytes 1179680 | tf_op jit(solution)/shard_map/ppermute | solution.py:375
  190.6 9.7 %attend_far.1 = (bf16[512,576]{1,0:T(8,128)(2,1)}, f32[2,2,4,256]{3,2,1,0:T(4,128)}) custom-call(s32[1]{0:T(128)} %get-tuple-element.109.flag, bf16[1536,1792]{1,0:T(8,128)(2,1)} %copy-done.48, bf16[512,1152]{1,0:T(8,128)(2,1)} %collective-permute-done.10.refs_1_), custom_call_target="tpu_custom_call" | custom-call | flops 4294967296 | bytes 4194304 | tf_op jit(solution)/shard_map/attend_far/pallas_call | solution.py:497
  219.5 11.1 %convert_reduce_fusion.2 = (f32[1536]{0:T(1024)S(1)}, bf16[1536,1152]{1,0:T(8,128)(2,1)S(1)}, f32[1536,1152]{1,0:T(8,128)}, f32[1536,1152]{1,0:T(8,128)}) fusion(f32[6,1152]{1,0:T(8,128)S(1)} %get-tuple-element.107, bf16[1536,1152]{1,0:T(8,128)(2,1)} %copy-done.1, f32[1152]{0:T(1024)S(1)} %copy-done.66, bf16[1152,1152]{1,0:T(8,128)(2,1)S(1)} %copy-done.12, ...), kind=kOutput, calls=%fused_computation.22 | convolution fusion | flops 4096326144 | bytes 27465216 | tf_op jit(solution)/shard_map/dot_general | solution.py:397
  235.4 17.1 %convolution_add_fusion = f32[1536,2304]{1,0:T(8,128)} fusion(bf16[1536,1152]{1,0:T(8,128)(2,1)S(1)} %get-tuple-element.64, f32[2304]{0:T(1024)S(1)} %copy-done.69, bf16[576,1152]{1,0:T(8,128)(2,1)S(1)} %copy-done.43, bf16[576,1152]{1,0:T(8,128)(2,1)S(1)} %copy-done.42, bf16[1152,1152]{1,0:T(8,128)(2,1)S(1)} %copy-done.46), kind=kOutput, calls=%fused_computation.14 | convolution fusion | flops 8173191168 | bytes 23012352 | tf_op jit(solution)/shard_map/dot_general | solution.py:401
  252.5 13.4 %convolution_convert_fusion = bf16[1152,2304]{1,0:T(8,128)(2,1)S(1)} fusion(bf16[1536,1152]{1,0:T(8,128)(2,1)S(1)} %copy-done.36, f32[1536,2304]{1,0:T(8,128)} %convolution_add_fusion), kind=kOutput, calls=%fused_computation.16 | convolution fusion | flops 8188231680 | bytes 23003136 | tf_op jit(solution)/shard_map/dot_general | solution.py:405
  275.1 25.5 %convert_reduce_fusion = (f32[2304]{0:T(1024)S(1)}, bf16[1536,2304]{1,0:T(8,128)(2,1)}) fusion(f32[1536,2304]{1,0:T(8,128)} %convolution_add_fusion, bf16[1536,1152]{1,0:T(8,128)(2,1)S(1)} %copy-done.36, bf16[576,1152]{1,0:T(8,128)(2,1)S(1)} %copy-done.41, bf16[576,1152]{1,0:T(8,128)(2,1)S(1)} %copy-done.40, bf16[1152,1152]{1,0:T(8,128)(2,1)} %all-gather.8.cloned.1.call-done), kind=kOutput, calls=%fused_computation.12 | convolution fusion | flops 8243968000 | bytes 30090240 | tf_op jit(solution)/shard_map/dot_general | solution.py:401
  302.4 13.2 %convolution_convert_fusion.1 = bf16[1152,2304]{1,0:T(8,128)(2,1)} fusion(bf16[1536,1152]{1,0:T(8,128)(2,1)S(1)} %get-tuple-element.64, bf16[1536,2304]{1,0:T(8,128)(2,1)} %get-tuple-element.114), kind=kOutput, calls=%fused_computation.17 | convolution fusion | flops 8156381184 | bytes 15925248 | tf_op jit(solution)/shard_map/dot_general | solution.py:405
  315.6 11.7 %convolution_convert_fusion.4 = bf16[1536,1152]{1,0:T(8,128)(2,1)S(1)} fusion(bf16[1536,2304]{1,0:T(8,128)(2,1)} %get-tuple-element.114, bf16[576,1152]{1,0:T(8,128)(2,1)S(1)} %copy-done.43, bf16[576,1152]{1,0:T(8,128)(2,1)S(1)} %copy-done.42, bf16[1152,1152]{1,0:T(8,128)(2,1)S(1)} %copy-done.46), kind=kOutput, calls=%fused_computation.29 | convolution fusion | flops 8171421696 | bytes 15925248 | tf_op jit(solution)/shard_map/dot_general | solution.py:397
  336.2 20.6 %convolution_convert_fusion.5 = bf16[1536,1152]{1,0:T(8,128)(2,1)} fusion(bf16[576,1152]{1,0:T(8,128)(2,1)} %get-tuple-element.70, bf16[576,1152]{1,0:T(8,128)(2,1)} %get-tuple-element.69, bf16[1152,1152]{1,0:T(8,128)(2,1)} %all-gather.8.cloned.1.call-done, f32[1536,2304]{1,0:T(8,128)} %convolution_add_fusion), kind=kOutput, calls=%fused_computation.30 | convolution fusion | flops 8203272192 | bytes 23003136 | tf_op jit(solution)/shard_map/dot_general | solution.py:397
  384.8 29.4 %collective-permute-done.21 = bf16[768,1152]{1,0:T(8,128)(2,1)} collective-permute-done((bf16[768,1152]{1,0:T(8,128)(2,1)}, bf16[768,1152]{1,0:T(8,128)(2,1)}, u32[]{:S(2)}, u32[]{:S(2)}) %collective-permute-start.21) | collective-permute-done | bytes 1769504 | tf_op jit(solution)/shard_map/ppermute | solution.py:375
  414.3 6.9 convert_multiply_fusion.3
  466.4 14.1 %attend_back_far.1 = (bf16[512,1792]{1,0:T(8,128)(2,1)}, bf16[512,1152]{1,0:T(8,128)(2,1)}) custom-call(s32[1]{0:T(128)} %get-tuple-element.109.flag, bf16[1536,1792]{1,0:T(8,128)(2,1)} %copy-done.48, bf16[512,1152]{1,0:T(8,128)(2,1)} %collective-permute-done.10.refs_1_, bf16[1536,576]{1,0:T(8,128)(2,1)} %fusion.56.refs_1_.refs_2_, ...), custom_call_target="tpu_custom_call" | custom-call | flops 10737418240 | bytes 8388608 | tf_op jit(solution)/shard_map/attend_back_far/pallas_call | solution.py:613
  485.5 19.7 %attend_back_near.1 = bf16[1024,1792]{1,0:T(8,128)(2,1)} custom-call(s32[1]{0:T(128)} %get-tuple-element.108.flag, bf16[1536,1792]{1,0:T(8,128)(2,1)} %copy-done.48, bf16[1536,576]{1,0:T(8,128)(2,1)} %fusion.56.refs_1_.refs_2_, bf16[1024,576]{1,0:T(8,128)(2,1)} %get-tuple-element.20.refs_2_, f32[2,4,4,256]{3,2,1,0:T(4,128)} %get-tuple-element.23.refs_3_), custom_call_target="tpu_custom_call" | custom-call | flops 21474836480 | bytes 16777216 | tf_op jit(solution)/shard_map/attend_back_near/pallas_call | solution.py:613
  510.4 25.0 %collective-permute-done.25 = bf16[512,1152]{1,0:T(8,128)(2,1)} collective-permute-done((bf16[512,1152]{1,0:T(8,128)(2,1)}, bf16[512,1152]{1,0:T(8,128)(2,1)}, u32[]{:S(2)}, u32[]{:S(2)}) %collective-permute-start.25) | collective-permute-done | bytes 1179680 | tf_op jit(solution)/shard_map/ppermute | solution.py:375
  550.3 7.4 convolution_convert_fusion.3
  560.2 11.5 %fusion.134 = (bf16[1536,1152]{1,0:T(8,128)(2,1)}, f32[1536,1152]{1,0:T(8,128)S(1)}) fusion(bf16[576,896]{1,0:T(8,128)(2,1)} %copy-done.45, bf16[576,896]{1,0:T(8,128)(2,1)} %copy-done.44, bf16[1152,896]{1,0:T(8,128)(2,1)} %all-gather.4.cloned.1.call-done, bf16[512,1792]{1,0:T(8,128)(2,1)S(1)} %add_convert_fusion.1, bf16[1024,1792]{1,0:T(8,128)(2,1)S(1)} %copy-done.33), kind=kOutput, calls=%fused_computation.325 | convolution fusion | flops 6366953472 | bytes 20250624 | tf_op jit(solution)/shard_map/dot_general | solution.py:397
  599.6 36.6 %collective-permute-done.29 = f32[12,1152]{1,0:T(8,128)S(1)} collective-permute-done((f32[12,1152]{1,0:T(8,128)S(1)}, f32[12,1152]{1,0:T(8,128)S(1)}, u32[]{:S(2)}, u32[]{:S(2)}) %collective-permute-start.29) | collective-permute-done | bytes 55328 | tf_op jit(solution)/shard_map/ppermute | solution.py:375
  645.9 32.3 %collective-permute-done.50 = bf16[2,144,288]{2,1,0:T(8,128)(2,1)S(1)} collective-permute-done((bf16[2,144,288]{2,1,0:T(8,128)(2,1)S(1)}, bf16[2,144,288]{2,1,0:T(8,128)(2,1)S(1)}, u32[]{:S(2)}, u32[]{:S(2)}) %collective-permute-start.50) | collective-permute-done | bytes 165920 | tf_op jit(solution)/shard_map/ppermute | solution.py:375
  689.9 7.6 fusion.44
  702.7 9.5 %collective-permute-done.54 = bf16[2,144,1152]{2,1,0:T(8,128)(2,1)} collective-permute-done((bf16[2,144,1152]{2,1,0:T(8,128)(2,1)}, bf16[2,144,1152]{2,1,0:T(8,128)(2,1)}, u32[]{:S(2)}, u32[]{:S(2)}) %collective-permute-start.54) | collective-permute-done | bytes 663584 | tf_op jit(solution)/shard_map/ppermute | solution.py:375
  713.4 8.8 %collective-permute-done.33 = f32[26,1152]{1,0:T(8,128)S(1)} collective-permute-done((f32[26,1152]{1,0:T(8,128)S(1)}, f32[26,1152]{1,0:T(8,128)S(1)}, u32[]{:S(2)}, u32[]{:S(2)}) %collective-permute-start.33) | collective-permute-done | bytes 119840 | tf_op jit(solution)/shard_map/ppermute | solution.py:375
  730.9 24.7 %collective-permute-done.35 = f32[26,1152]{1,0:T(8,128)S(1)} collective-permute-done((f32[26,1152]{1,0:T(8,128)S(1)}, f32[26,1152]{1,0:T(8,128)S(1)}, u32[]{:S(2)}, u32[]{:S(2)}) %collective-permute-start.35) | collective-permute-done | bytes 119840 | tf_op jit(solution)/shard_map/ppermute | solution.py:375
  756.6 6.7 collective-permute-done.36
  771.0 19.1 %collective-permute-done.41 = bf16[2,144,896]{2,1,0:T(8,128)(2,1)S(1)} collective-permute-done((bf16[2,144,896]{2,1,0:T(8,128)(2,1)S(1)}, bf16[2,144,896]{2,1,0:T(8,128)(2,1)S(1)}, u32[]{:S(2)}, u32[]{:S(2)}) %collective-permute-start.41) | collective-permute-done | bytes 516128 | tf_op jit(solution)/shard_map/ppermute | solution.py:375
  791.6 6.8 collective-permute-done.42
  (473 shorter events, 304.0 us)
Async XLA Ops:
  7.2 68.5 %all-gather.4.cloned.1.call-start = ((), (), s32[]{:S(2)}) async-start(), calls=%async_computation | async-start | bytes 2322432 | tf_op jit(solution)/shard_map/all_gather | solution.py:717
  9.4 93.1 %all-gather.6.cloned.1.call-start = ((), (), s32[]{:S(2)}) async-start(), calls=%async_computation.1 | async-start | bytes 2985984 | tf_op jit(solution)/shard_map/all_gather | solution.py:717
  10.2 106.1 %all-gather.8.cloned.1.call-start = ((), (), s32[]{:S(2)}) async-start(), calls=%async_computation.2 | async-start | bytes 2985984 | tf_op jit(solution)/shard_map/all_gather | solution.py:717
  10.3 79.2 %collective-permute-start = (bf16[768,1152]{1,0:T(8,128)(2,1)}, bf16[768,1152]{1,0:T(8,128)(2,1)}, u32[]{:S(2)}, u32[]{:S(2)}) collective-permute-start(bf16[768,1152]{1,0:T(8,128)(2,1)} %param.14), channel_id=1, source_target_pairs={{0,1},{1,0},{2,3},{3,2},{4,5},{5,4},{6,7},{7,6},{8,9},{9,8},{10,11... | collective-permute-start | bytes 5308424 | tf_op jit(solution)/shard_map/ppermute | solution.py:375
  14.3 32.3 %collective-permute-start.1 = (f32[6,6,288]{2,0,1:T(8,128)S(1)}, f32[6,6,288]{2,0,1:T(8,128)S(1)}, u32[]{:S(2)}, u32[]{:S(2)}) collective-permute-start(f32[6,6,288]{2,0,1:T(8,128)S(1)} %fusion.80), channel_id=1, source_target_pairs={{0,4},{4,0},{8,12},{12,8},{16,20},{20,16},{24,28},{28,24},{1,5},{5... | collective-permute-start | bytes 124424 | tf_op jit(solution)/shard_map/ppermute | solution.py:375
  14.4 32.3 %collective-permute-start.8 = (bf16[2,288]{1,0:T(2,128)(2,1)}, bf16[2,288]{1,0:T(2,128)(2,1)S(1)}, u32[]{:S(2)}, u32[]{:S(2)}) collective-permute-start(bf16[2,288]{1,0:T(2,128)(2,1)} %param.20), channel_id=1, source_target_pairs={{0,2},{1,3},{2,0},{3,1},{4,6},{5,7},{6,4},{7,5},{8,10},{9,11},{10,... | collective-permute-start | bytes 3464 | tf_op jit(solution)/shard_map/ppermute | solution.py:375
  89.5 58.6 %collective-permute-start.15 = (bf16[576,576]{1,0:T(8,128)(2,1)}, bf16[576,576]{1,0:T(8,128)(2,1)}, u32[]{:S(2)}, u32[]{:S(2)}) collective-permute-start(bf16[576,576]{1,0:T(8,128)(2,1)} %collective-permute-done.14), channel_id=1, source_target_pairs={{0,4},{4,0},{8,12},{12,8},{16,20},{20,16},{24,28},{28,24},{1,5},{5... | collective-permute-start | bytes 1990664 | tf_op jit(solution)/shard_map/ppermute | solution.py:375
  89.5 70.9 %collective-permute-start.22 = (bf16[768,1152]{1,0:T(8,128)(2,1)}, bf16[768,1152]{1,0:T(8,128)(2,1)}, u32[]{:S(2)}, u32[]{:S(2)}) collective-permute-start(bf16[768,1152]{1,0:T(8,128)(2,1)} %param.27), channel_id=1, source_target_pairs={{0,1},{1,0},{2,3},{3,2},{4,5},{5,4},{6,7},{7,6},{8,9},{9,8},{10,11... | collective-permute-start | bytes 5308424 | tf_op jit(solution)/shard_map/ppermute | solution.py:375
  105.1 44.5 %collective-permute-start.16 = (bf16[576,1152]{1,0:T(8,128)(2,1)}, bf16[576,1152]{1,0:T(8,128)(2,1)}, u32[]{:S(2)}, u32[]{:S(2)}) collective-permute-start(bf16[576,1152]{1,0:T(8,128)(2,1)} %constant_dynamic-slice_fusion.12), channel_id=1, source_target_pairs={{0,2},{1,3},{2,0},{3,1},{4,6},{5,7},{6,4},{7,5},{8,10},{9,11},{10,... | collective-permute-start | bytes 3981320 | tf_op jit(solution)/shard_map/ppermute | solution.py:375
  119.0 53.4 %collective-permute-start.19 = (bf16[576,1152]{1,0:T(8,128)(2,1)}, bf16[576,1152]{1,0:T(8,128)(2,1)}, u32[]{:S(2)}, u32[]{:S(2)}) collective-permute-start(bf16[576,1152]{1,0:T(8,128)(2,1)} %constant_dynamic-slice_fusion.11), channel_id=1, source_target_pairs={{0,2},{1,3},{2,0},{3,1},{4,6},{5,7},{6,4},{7,5},{8,10},{9,11},{10,... | collective-permute-start | bytes 3981320 | tf_op jit(solution)/shard_map/ppermute | solution.py:375
  131.4 59.3 %collective-permute-start.10 = (bf16[512,1152]{1,0:T(8,128)(2,1)}, bf16[512,1152]{1,0:T(8,128)(2,1)}, u32[]{:S(2)}, u32[]{:S(2)}) collective-permute-start(bf16[512,1152]{1,0:T(8,128)(2,1)} %pad_maximum_fusion.5), channel_id=1, source_target_pairs={{0,2},{1,3},{2,0},{3,1},{4,6},{5,7},{6,4},{7,5},{8,10},{9,11},{10,... | collective-permute-start | bytes 3538952 | tf_op jit(solution)/shard_map/ppermute | solution.py:375
  148.1 56.2 %collective-permute-start.9 = (bf16[1024,576]{0,1:T(8,128)(2,1)}, bf16[1024,576]{0,1:T(8,128)(2,1)}, u32[]{:S(2)}, u32[]{:S(2)}) collective-permute-start(bf16[1024,576]{0,1:T(8,128)(2,1)} %copy.32), channel_id=1, source_target_pairs={{0,1},{1,0},{2,3},{3,2},{4,5},{5,4},{6,7},{7,6},{8,9},{9,8},{10,11... | collective-permute-start | bytes 3538952 | tf_op jit(solution)/shard_map/ppermute | solution.py:375
  149.5 58.7 %collective-permute-start.17 = (bf16[576,1152]{1,0:T(8,128)(2,1)}, bf16[576,1152]{1,0:T(8,128)(2,1)}, u32[]{:S(2)}, u32[]{:S(2)}) collective-permute-start(bf16[576,1152]{1,0:T(8,128)(2,1)} %collective-permute-done.16), channel_id=1, source_target_pairs={{0,4},{4,0},{8,12},{12,8},{16,20},{20,16},{24,28},{28,24},{1,5},{5... | collective-permute-start | bytes 3981320 | tf_op jit(solution)/shard_map/ppermute | solution.py:375
  172.4 39.3 %collective-permute-start.20 = (bf16[576,1152]{1,0:T(8,128)(2,1)}, bf16[576,1152]{1,0:T(8,128)(2,1)}, u32[]{:S(2)}, u32[]{:S(2)}) collective-permute-start(bf16[576,1152]{1,0:T(8,128)(2,1)} %collective-permute-done.19), channel_id=1, source_target_pairs={{0,4},{4,0},{8,12},{12,8},{16,20},{20,16},{24,28},{28,24},{1,5},{5... | collective-permute-start | bytes 3981320 | tf_op jit(solution)/shard_map/ppermute | solution.py:375
  270.2 174.3 %collective-permute-start.60 = (bf16[4,144,2304]{2,1,0:T(8,128)(2,1)}, bf16[4,144,2304]{2,1,0:T(8,128)(2,1)}, u32[]{:S(2)}, u32[]{:S(2)}) collective-permute-start(bf16[4,144,2304]{2,1,0:T(8,128)(2,1)} %dynamic-slice_bitcast_fusion), channel_id=1, source_target_pairs={{0,4},{4,0},{8,12},{12,8},{16,20},{20,16},{24,28},{28,24},{1,5},{5... | collective-permute-start | bytes 7962632 | tf_op jit(solution)/shard_map/ppermute | solution.py:375
  300.7 35.5 %collective-permute-start.56 = (f32[1152]{0:T(1024)S(1)}, f32[1152]{0:T(1024)S(1)}, u32[]{:S(2)}, u32[]{:S(2)}) collective-permute-start(f32[1152]{0:T(1024)S(1)} %slice.280), channel_id=1, source_target_pairs={{0,2},{1,3},{2,0},{3,1},{4,6},{5,7},{6,4},{7,5},{8,10},{9,11},{10,... | collective-permute-start | bytes 13832 | tf_op jit(solution)/shard_map/ppermute | solution.py:375
  335.8 41.7 %collective-permute-start.23 = (bf16[768,1152]{1,0:T(8,128)(2,1)}, bf16[768,1152]{1,0:T(8,128)(2,1)S(1)}, u32[]{:S(2)}, u32[]{:S(2)}) collective-permute-start(bf16[768,1152]{1,0:T(8,128)(2,1)} %slice.257), channel_id=1, source_target_pairs={{0,1},{1,0},{2,3},{3,2},{4,5},{5,4},{6,7},{7,6},{8,9},{9,8},{10,11... | collective-permute-start | bytes 5308424 | tf_op jit(solution)/shard_map/ppermute | solution.py:375
  364.2 50.1 %collective-permute-start.21 = (bf16[768,1152]{1,0:T(8,128)(2,1)}, bf16[768,1152]{1,0:T(8,128)(2,1)}, u32[]{:S(2)}, u32[]{:S(2)}) collective-permute-start(bf16[768,1152]{1,0:T(8,128)(2,1)} %slice.255), channel_id=1, source_target_pairs={{0,1},{1,0},{2,3},{3,2},{4,5},{5,4},{6,7},{7,6},{8,9},{9,8},{10,11... | collective-permute-start | bytes 5308424 | tf_op jit(solution)/shard_map/ppermute | solution.py:375
  372.3 77.4 %collective-permute-start.52 = (bf16[4,144,2304]{2,1,0:T(8,128)(2,1)}, bf16[4,144,2304]{2,1,0:T(8,128)(2,1)}, u32[]{:S(2)}, u32[]{:S(2)}) collective-permute-start(bf16[4,144,2304]{2,1,0:T(8,128)(2,1)} %dynamic-slice_bitcast_fusion.1), channel_id=1, source_target_pairs={{0,4},{4,0},{8,12},{12,8},{16,20},{20,16},{24,28},{28,24},{1,5},{5... | collective-permute-start | bytes 7962632 | tf_op jit(solution)/shard_map/ppermute | solution.py:375
  429.8 51.0 %collective-permute-start.47 = (bf16[4,144,1152]{2,1,0:T(8,128)(2,1)}, bf16[4,144,1152]{2,1,0:T(8,128)(2,1)}, u32[]{:S(2)}, u32[]{:S(2)}) collective-permute-start(bf16[4,144,1152]{2,1,0:T(8,128)(2,1)} %dynamic-slice_bitcast_fusion.3), channel_id=1, source_target_pairs={{0,4},{4,0},{8,12},{12,8},{16,20},{20,16},{24,28},{28,24},{1,5},{5... | collective-permute-start | bytes 3981320 | tf_op jit(solution)/shard_map/ppermute | solution.py:375
  449.4 147.1 %collective-permute-start.61 = (bf16[4,144,1152]{2,1,0:T(8,128)(2,1)}, bf16[4,144,1152]{2,1,0:T(8,128)(2,1)}, u32[]{:S(2)}, u32[]{:S(2)}) collective-permute-start(bf16[4,144,1152]{2,1,0:T(8,128)(2,1)} %slice.282), channel_id=1, source_target_pairs={{0,2},{1,3},{2,0},{3,1},{4,6},{5,7},{6,4},{7,5},{8,10},{9,11},{10,... | collective-permute-start | bytes 3981320 | tf_op jit(solution)/shard_map/ppermute | solution.py:375
  453.3 187.9 %collective-permute-start.53 = (bf16[4,144,1152]{2,1,0:T(8,128)(2,1)}, bf16[4,144,1152]{2,1,0:T(8,128)(2,1)}, u32[]{:S(2)}, u32[]{:S(2)}) collective-permute-start(bf16[4,144,1152]{2,1,0:T(8,128)(2,1)} %slice.278), channel_id=1, source_target_pairs={{0,2},{1,3},{2,0},{3,1},{4,6},{5,7},{6,4},{7,5},{8,10},{9,11},{10,... | collective-permute-start | bytes 3981320 | tf_op jit(solution)/shard_map/ppermute | solution.py:375
  480.5 54.9 %collective-permute-start.25 = (bf16[512,1152]{1,0:T(8,128)(2,1)}, bf16[512,1152]{1,0:T(8,128)(2,1)}, u32[]{:S(2)}, u32[]{:S(2)}) collective-permute-start(bf16[512,1152]{1,0:T(8,128)(2,1)} %get-tuple-element.26), channel_id=1, source_target_pairs={{0,2},{1,3},{2,0},{3,1},{4,6},{5,7},{6,4},{7,5},{8,10},{9,11},{10,... | collective-permute-start | bytes 3538952 | tf_op jit(solution)/shard_map/ppermute | solution.py:375
  508.6 130.2 %collective-permute-start.49 = (bf16[4,144,288]{2,1,0:T(8,128)(2,1)}, bf16[4,144,288]{2,1,0:T(8,128)(2,1)}, u32[]{:S(2)}, u32[]{:S(2)}) collective-permute-start(bf16[4,144,288]{2,1,0:T(8,128)(2,1)} %slice.275), channel_id=1, source_target_pairs={{0,2},{1,3},{2,0},{3,1},{4,6},{5,7},{6,4},{7,5},{8,10},{9,11},{10,... | collective-permute-start | bytes 995336 | tf_op jit(solution)/shard_map/ppermute | solution.py:375
  560.2 163.8 %collective-permute-start.39 = (bf16[4,144,1792]{2,1,0:T(8,128)(2,1)}, bf16[4,144,1792]{2,1,0:T(8,128)(2,1)}, u32[]{:S(2)}, u32[]{:S(2)}) collective-permute-start(bf16[4,144,1792]{2,1,0:T(8,128)(2,1)} %dynamic-slice_bitcast_fusion.2), channel_id=1, source_target_pairs={{0,4},{4,0},{8,12},{12,8},{16,20},{20,16},{24,28},{28,24},{1,5},{5... | collective-permute-start | bytes 6193160 | tf_op jit(solution)/shard_map/ppermute | solution.py:375
  594.8 90.8 %collective-permute-start.26 = (bf16[768,1152]{1,0:T(8,128)(2,1)}, bf16[768,1152]{1,0:T(8,128)(2,1)}, u32[]{:S(2)}, u32[]{:S(2)}) collective-permute-start(bf16[768,1152]{1,0:T(8,128)(2,1)} %slice.263), channel_id=1, source_target_pairs={{0,1},{1,0},{2,3},{3,2},{4,5},{5,4},{6,7},{7,6},{8,9},{9,8},{10,11... | collective-permute-start | bytes 5308424 | tf_op jit(solution)/shard_map/ppermute | solution.py:375
  596.5 39.7 %collective-permute-start.29 = (f32[12,1152]{1,0:T(8,128)S(1)}, f32[12,1152]{1,0:T(8,128)S(1)}, u32[]{:S(2)}, u32[]{:S(2)}) collective-permute-start(f32[12,1152]{1,0:T(8,128)S(1)} %add.524), channel_id=1, source_target_pairs={{0,1},{1,0},{2,3},{3,2},{4,5},{5,4},{6,7},{7,6},{8,9},{9,8},{10,11... | collective-permute-start | bytes 165896 | tf_op jit(solution)/shard_map/ppermute | solution.py:375
  636.1 47.9 %collective-permute-start.62 = (bf16[2,144,1152]{2,1,0:T(8,128)(2,1)}, bf16[2,144,1152]{2,1,0:T(8,128)(2,1)}, u32[]{:S(2)}, u32[]{:S(2)}) collective-permute-start(bf16[2,144,1152]{2,1,0:T(8,128)(2,1)} %dynamic-slice_bitcast_fusion.4), channel_id=1, source_target_pairs={{0,16},{4,20},{8,24},{12,28},{16,0},{20,4},{24,8},{28,12},{1,17},{... | collective-permute-start | bytes 1990664 | tf_op jit(solution)/shard_map/ppermute | solution.py:375
  641.1 37.1 %collective-permute-start.50 = (bf16[2,144,288]{2,1,0:T(8,128)(2,1)S(1)}, bf16[2,144,288]{2,1,0:T(8,128)(2,1)S(1)}, u32[]{:S(2)}, u32[]{:S(2)}) collective-permute-start(bf16[2,144,288]{2,1,0:T(8,128)(2,1)S(1)} %dynamic-slice_bitcast_fusion.10), channel_id=1, source_target_pairs={{0,16},{4,20},{8,24},{12,28},{16,0},{20,4},{24,8},{28,12},{1,17},{... | collective-permute-start | bytes 497672 | tf_op jit(solution)/shard_map/ppermute | solution.py:375
  643.3 36.5 %collective-permute-start.31 = (f32[12,1152]{1,0:T(8,128)S(1)}, f32[12,1152]{1,0:T(8,128)S(1)}, u32[]{:S(2)}, u32[]{:S(2)}) collective-permute-start(f32[12,1152]{1,0:T(8,128)S(1)} %add.526), channel_id=1, source_target_pairs={{0,16},{4,20},{8,24},{12,28},{16,0},{20,4},{24,8},{28,12},{1,17},{... | collective-permute-start | bytes 165896 | tf_op jit(solution)/shard_map/ppermute | solution.py:375
  679.9 32.3 %collective-permute-start.54 = (bf16[2,144,1152]{2,1,0:T(8,128)(2,1)}, bf16[2,144,1152]{2,1,0:T(8,128)(2,1)}, u32[]{:S(2)}, u32[]{:S(2)}) collective-permute-start(bf16[2,144,1152]{2,1,0:T(8,128)(2,1)} %dynamic-slice_bitcast_fusion.5), channel_id=1, source_target_pairs={{0,16},{4,20},{8,24},{12,28},{16,0},{20,4},{24,8},{28,12},{1,17},{... | collective-permute-start | bytes 1990664 | tf_op jit(solution)/shard_map/ppermute | solution.py:375
  727.7 35.7 %collective-permute-start.40 = (bf16[4,144,896]{2,1,0:T(8,128)(2,1)}, bf16[4,144,896]{2,1,0:T(8,128)(2,1)}, u32[]{:S(2)}, u32[]{:S(2)}) collective-permute-start(bf16[4,144,896]{2,1,0:T(8,128)(2,1)} %slice.266), channel_id=1, source_target_pairs={{0,2},{1,3},{2,0},{3,1},{4,6},{5,7},{6,4},{7,5},{8,10},{9,11},{10,... | collective-permute-start | bytes 3096584 | tf_op jit(solution)/shard_map/ppermute | solution.py:375
  (118 other events, 1582.7 us)
Sparse Core Ops, SparseCore 0:
  10.3 36.1 all-gather.3
  48.1 33.3 all-gather.5
  83.2 33.1 all-gather.7
